TPU v7x, 256 devices: a whole 4x4x8 slice. The times are simulated.
256 devices in a mesh: tile: 64 (over y, z, x_lo), sub: 4 (over x_hi, core).
Axes of the slice: x: 4 (x_hi: 2, x_lo: 2; x = x_hi * 2 + x_lo), y: 4, z: 8, core: 2. Of those that a mesh axis runs over, the one named last changes fastest.
Arguments:
- water_state: float32 [3, 512, 16384], P(None, 'tile', 'sub'), may hold values from -6 to 6
- water_coef: float32 [2, 512, 16384], P(None, 'tile', 'sub'), may hold values from 0.15 to 0.6
- steel_state: float32 [5, 1024, 16384], P(None, 'tile', 'sub'), may hold values from -6 to 6
- steel_coef: float32 [5, 1024, 16384], P(None, 'tile', 'sub'), may hold values from 0.15 to 0.6
- coupling: float32 [9], replicated, may hold values from 0.3 to 1.5
- water_cell: int32 [192, 1024], P('tile', 'sub'), may hold values from 0 to 32767, as said below
- stencil_code: int32 [192, 1024], P('tile', 'sub'), may hold values from 0 to 8
- link_count: int32 [192, 4], P('tile', 'sub'), may hold values from 0 to 256, as said below
- steel_cell: int32 [192, 1024], P('tile', 'sub'), may hold values from 4097 to 61438, as said below
Outputs:
- water_next: float32 [3, 512, 16384], P(None, 'tile', 'sub')
- steel_next: float32 [5, 1024, 16384], P(None, 'tile', 'sub')
Inputs may be any that keep to these rules, and one draw needn't show every extreme that they name: `link_count`: entry [a * 3 + j, c] is the number of live leading slots of the list from water device (a, c) to steel device (a + j - 1, c); it is 0 where that tile does not exist, and for every water device one of its lists is full. `water_cell`: slots follow the interface curve: a few rows of each column near a profile that varies along the columns. `steel_cell`: entry [b * 3 + m, c * 256 + k] is row * 4096 + column in the block of steel device (b, c) that slot k of the list from water device (b + m - 1, c) reaches; it never lies in a block's outermost rows or columns.
All inputs are finite; a program needn't handle non-finite values.
Results may differ from a plain program's by a relative error of at most 0.00002.
Values sent between devices are 32-bit elements; how exact they have to be, the bound alone decides.
A program may use at most 64 MiB of HBM per device.

v0:
```python
import jax
import jax.numpy as jnp
from jax import lax
from jax.sharding import PartitionSpec as P

STEPS = 3


def padded(array, sides, width):
    for axis, dim in sides:
        size, length = (lax.axis_size(axis), array.shape[dim])
        up = [(i, (i + 1) % size) for i in range(size - 1)]
        down = [(j, i) for i, j in up]
        last = lax.slice_in_dim(array, length - width, length, axis=dim)
        initial = lax.slice_in_dim(array, 0, width, axis=dim)
        before = lax.ppermute(last, axis, up)
        after = lax.ppermute(initial, axis, down)
        array = jnp.concatenate([before, array, after], axis=dim)
    return array


def centre_rows(extended):
    return 0.5 * (extended[2:, 1:-1] - extended[:-2, 1:-1])


def centre_columns(extended):
    return 0.5 * (extended[1:-1, 2:] - extended[1:-1, :-2])


def inside_grid(rows, columns):
    tile_at = lax.axis_index("tile")
    tile_count = lax.axis_size("tile")
    sub_at = lax.axis_index("sub")
    sub_count = lax.axis_size("sub")
    row_index = jnp.arange(rows + 2)
    column_index = jnp.arange(columns + 2)
    row_inside = ((row_index > 0) | (tile_at > 0)) & (
        (row_index < rows + 1) | (tile_at < tile_count - 1)
    )
    column_inside = ((column_index > 0) | (sub_at > 0)) & (
        (column_index < columns + 1) | (sub_at < sub_count - 1)
    )
    return row_inside[:, None] & column_inside[None, :]


def water_update(state, coef, feeding):
    inside = inside_grid(state.shape[1], state.shape[2])
    stacked = jnp.concatenate([state, coef[0:1]], axis=0)
    extended = padded(stacked, (("tile", 1), ("sub", 2)), 2)
    buoyancy = extended[3, 1:-1, 1:-1]
    velocity_x = jnp.where(
        inside, extended[1, 1:-1, 1:-1] - buoyancy * centre_rows(extended[0]), 0.0
    )
    velocity_z = jnp.where(
        inside, extended[2, 1:-1, 1:-1] - buoyancy * centre_columns(extended[0]), 0.0
    )
    pressure = state[0] - coef[1] * (centre_rows(velocity_x) + centre_columns(velocity_z)) + feeding
    return jnp.stack([pressure, velocity_x[1:-1, 1:-1], velocity_z[1:-1, 1:-1]])


def stress_update(state, coef, velocity_x, velocity_z):
    stress_xx = state[2] + coef[1] * centre_rows(velocity_x) + coef[2] * centre_columns(velocity_z)
    stress_zz = state[3] + coef[2] * centre_rows(velocity_x) + coef[3] * centre_columns(velocity_z)
    stress_xz = state[4] + coef[4] * (centre_columns(velocity_x) + centre_rows(velocity_z))
    return jnp.stack(
        [velocity_x[1:-1, 1:-1], velocity_z[1:-1, 1:-1], stress_xx, stress_zz, stress_xz]
    )


def steel_update(state, coef, loading):
    stresses = padded(state[2:5], (("tile", 1), ("sub", 2)), 1)
    moved_x = state[0] + coef[0] * (centre_rows(stresses[0]) + centre_columns(stresses[2]))
    moved_z = state[1] + coef[0] * (
        centre_rows(stresses[2]) + centre_columns(stresses[1]) - loading
    )
    extended = padded(jnp.stack([moved_x, moved_z]), (("tile", 1), ("sub", 2)), 1)
    velocity_x = extended[0]
    velocity_z = extended[1]
    return stress_update(state, coef, velocity_x, velocity_z)


def on_device(
    water_state,
    water_coef,
    steel_state,
    steel_coef,
    coupling,
    water_cell,
    stencil_code,
    link_count,
    steel_cell,
):
    water_rows = water_state.shape[1]
    water_columns = water_state.shape[2]
    steel_rows = steel_state.shape[1]
    steel_columns = steel_state.shape[2]
    slots = water_cell.shape[1]
    live = (jnp.arange(slots, dtype=jnp.int32)[None, :] < link_count).astype(jnp.float32)
    weight = jnp.zeros(stencil_code.shape, jnp.float32)
    for stencil in range(9):
        weight = weight + jnp.where(stencil_code == stencil, coupling[stencil], 0.0)
    factor = weight * live
    water_flat = water_cell.reshape(-1)
    steel_flat = steel_cell.reshape(-1)
    for time_step in range(STEPS):
        sample = water_state[0].reshape(-1)[water_flat].reshape(factor.shape) * factor
        beside = padded(sample, (("tile", 0),), 1)
        arriving = jnp.stack([beside[0], beside[2], beside[4]])
        loading = (
            jnp.zeros((steel_rows * steel_columns,), jnp.float32)
            .at[steel_flat]
            .add(arriving.reshape(-1))
        )
        steel_state = steel_update(
            steel_state, steel_coef, loading.reshape(steel_rows, steel_columns)
        )
        traction = steel_state[3].reshape(-1)[steel_flat].reshape(factor.shape)
        back = padded(traction, (("tile", 0),), 1)
        returning = jnp.stack([back[0], back[2], back[4]])
        feeding = (
            jnp.zeros((water_rows * water_columns,), jnp.float32)
            .at[water_flat]
            .add((returning * factor).reshape(-1))
        )
        water_state = water_update(
            water_state, water_coef, feeding.reshape(water_rows, water_columns)
        )
    return (water_state, steel_state)


def solution(mesh):
    in_specs = (
        P(None, "tile", "sub"),
        P(None, "tile", "sub"),
        P(None, "tile", "sub"),
        P(None, "tile", "sub"),
        P(),
        P("tile", "sub"),
        P("tile", "sub"),
        P("tile", "sub"),
        P("tile", "sub"),
    )
    out_specs = (P(None, "tile", "sub"), P(None, "tile", "sub"))
    return jax.shard_map(
        on_device, mesh=mesh, in_specs=in_specs, out_specs=out_specs, check_vma=False
    )
```

profile of v0, /device:TPU:25, one launch (start us, length us, event | category | flops | bytes accessed | tf_op | source)
XLA Modules:
  0.0 323.1 jit_solution(6336181813005315874)
XLA Ops:
  1.8 3.1 collective-permute-start.4
  4.9 7.4 %collective-permute-start.5 = (f32[3,1,4096]{2,1,0:T(1,128)S(1)}, f32[3,1,4096]{2,1,0:T(1,128)S(1)}, u32[]{:S(2)}, u32[]{:S(2)}) collective-permute-start(f32[3,1,4096]{2,1,0:T(1,128)S(1)} %get-tuple-element.23), channel_id=1, source_target_pairs={{4,0},{8,4},{12,8},{16,12},{20,16},{24,20},{28,24},{32,28},{36,32}... | collective-permute-start | bytes 147464 | tf_op jit(solution)/shard_map/ppermute | solution.py:17
  16.5 4.5 %gather_fusion = f32[768]{0:T(1024)S(1)} fusion(f32[32768]{0:T(1024)S(1)} %bitcast.250, s32[1024]{0:T(1024)S(1)} %get-tuple-element.110), kind=kCustom, calls=%fused_computation | custom fusion | bytes 9216 | tf_op jit(solution)/shard_map/gather | solution.py:106
  21.0 5.7 %fusion.126 = (f32[3,256]{1,0:T(4,128)S(1)}, f32[3,256]{1,0:T(4,128)S(1)}) fusion(f32[3,256]{1,0:T(4,128)S(1)} %reshape.143, f32[]{:T(128)} %bitcast.24, s32[3,256]{1,0:T(4,128)S(1)} %copy-done.32, f32[]{:T(128)} %bitcast.23, f32[]{:T(128)} %bitcast.22, f32[]{:T(128)} %bitcast.21, f32[]{:T(128)} %bitcast.20, f32[]{:T(128)} %bitcast.19, f32[]{:T(128)} %bitcast.18, ...), kind=kLoop, calls=%fused_computation.271 | loop fusion | flops 22272 | bytes 12336 | tf_op jit(solution)/shard_map/mul | solution.py:106
  28.6 6.4 %collective-permute-start.9 = (f32[1,256]{1,0:T(1,128)S(1)}, f32[1,256]{1,0:T(1,128)S(1)}, u32[]{:S(2)}, u32[]{:S(2)}) collective-permute-start(f32[1,256]{1,0:T(1,128)S(1)} %get-tuple-element.98), channel_id=1, source_target_pairs={{4,0},{8,4},{12,8},{16,12},{20,16},{24,20},{28,24},{32,28},{36,32}... | collective-permute-start | bytes 3080 | tf_op jit(solution)/shard_map/ppermute | solution.py:17
  37.7 6.4 %collective-permute-start.1 = (f32[4,2,4096]{2,1,0:T(2,128)}, f32[4,2,4096]{2,1,0:T(2,128)}, u32[]{:S(2)}, u32[]{:S(2)}) collective-permute-start(f32[4,2,4096]{2,1,0:T(2,128)} %get-tuple-element.72), channel_id=1, source_target_pairs={{4,0},{8,4},{12,8},{16,12},{20,16},{24,20},{28,24},{32,28},{36,32}... | collective-permute-start | bytes 393224 | tf_op jit(solution)/shard_map/ppermute | solution.py:17
  44.4 4.0 %collective-permute-start.7 = (f32[3,18,1]{2,1,0:T(8,128)S(1)}, f32[3,18,1]{2,1,0:T(8,128)S(1)}, u32[]{:S(2)}, u32[]{:S(2)}) collective-permute-start(f32[3,18,1]{2,1,0:T(8,128)S(1)} %get-tuple-element.37), channel_id=1, source_target_pairs={{1,0},{2,1},{3,2},{5,4},{6,5},{7,6},{9,8},{10,9},{11,10},{13,12},{... | collective-permute-start | bytes 656 | tf_op jit(solution)/shard_map/ppermute | solution.py:17
  48.4 4.3 %collective-permute-start.6 = (f32[3,18,1]{2,1,0:T(8,128)S(1)}, f32[3,18,1]{2,1,0:T(8,128)S(1)}, u32[]{:S(2)}, u32[]{:S(2)}) collective-permute-start(f32[3,18,1]{2,1,0:T(8,128)S(1)} %get-tuple-element.38), channel_id=1, source_target_pairs={{0,1},{1,2},{2,3},{4,5},{5,6},{6,7},{8,9},{9,10},{10,11},{12,13},{... | collective-permute-start | bytes 656 | tf_op jit(solution)/shard_map/ppermute | solution.py:16
  52.7 4.7 %scatter_custom_fusion = f32[65536]{0:T(1024)S(1)} fusion(s32[768]{0:T(1024)S(1)} %fusion.124, f32[768]{0:T(1024)S(1)} %reshape.210, f32[]{:T(128)} %constant.4.clone.1), kind=kCustom, calls=%fused_computation.230 | custom fusion | flops 768 | bytes 262148 | tf_op jit(solution)/shard_map/scatter-add | solution.py:112
  61.2 1.9 collective-permute-start.10
  63.1 6.4 %collective-permute-start.11 = (f32[2,1,4096]{2,1,0:T(1,128)S(1)}, f32[2,1,4096]{2,1,0:T(1,128)S(1)}, u32[]{:S(2)}, u32[]{:S(2)}) collective-permute-start(f32[2,1,4096]{2,1,0:T(1,128)S(1)} %get-tuple-element.70), channel_id=1, source_target_pairs={{4,0},{8,4},{12,8},{16,12},{20,16},{24,20},{28,24},{32,28},{36,32}... | collective-permute-start | bytes 98312 | tf_op jit(solution)/shard_map/ppermute | solution.py:17
  70.7 1.9 collective-permute-start.13
  72.6 5.1 %collective-permute-start.12 = (f32[2,18,1]{2,1,0:T(8,128)S(1)}, f32[2,18,1]{2,1,0:T(8,128)S(1)}, u32[]{:S(2)}, u32[]{:S(2)}) collective-permute-start(f32[2,18,1]{2,1,0:T(8,128)S(1)} %get-tuple-element.60), channel_id=1, source_target_pairs={{0,1},{1,2},{2,3},{4,5},{5,6},{6,7},{8,9},{9,10},{10,11},{12,13},{... | collective-permute-start | bytes 440 | tf_op jit(solution)/shard_map/ppermute | solution.py:16
  82.1 4.5 %gather_fusion.1 = f32[768]{0:T(1024)S(1)} fusion(f32[65536]{0:T(1024)S(1)} %bitcast.254, s32[1024]{0:T(1024)S(1)} %get-tuple-element.109), kind=kCustom, calls=%fused_computation.1 | custom fusion | bytes 9216 | tf_op jit(solution)/shard_map/gather | solution.py:117
  86.6 1.9 collective-permute-start.14
  88.5 6.7 %collective-permute-start.15 = (f32[1,256]{1,0:T(1,128)S(1)}, f32[1,256]{1,0:T(1,128)S(1)}, u32[]{:S(2)}, u32[]{:S(2)}) collective-permute-start(f32[1,256]{1,0:T(1,128)S(1)} %bitcast.286), channel_id=1, source_target_pairs={{4,0},{8,4},{12,8},{16,12},{20,16},{24,20},{28,24},{32,28},{36,32}... | collective-permute-start | bytes 3080 | tf_op jit(solution)/shard_map/ppermute | solution.py:17
  95.3 1.9 collective-permute-start.20
  97.2 6.4 %collective-permute-start.21 = (f32[3,1,4096]{2,1,0:T(1,128)S(1)}, f32[3,1,4096]{2,1,0:T(1,128)}, u32[]{:S(2)}, u32[]{:S(2)}) collective-permute-start(f32[3,1,4096]{2,1,0:T(1,128)S(1)} %get-tuple-element.58), channel_id=1, source_target_pairs={{4,0},{8,4},{12,8},{16,12},{20,16},{24,20},{28,24},{32,28},{36,32}... | collective-permute-start | bytes 147464 | tf_op jit(solution)/shard_map/ppermute | solution.py:17
  103.6 4.6 %scatter_custom_fusion.1 = f32[32768]{0:T(1024)S(1)} fusion(s32[768]{0:T(1024)S(1)} %fusion.123, f32[768]{0:T(1024)S(1)} %reshape.218, f32[]{:T(128)} %constant.4.clone.1), kind=kCustom, calls=%fused_computation.237 | custom fusion | flops 768 | bytes 131076 | tf_op jit(solution)/shard_map/scatter-add | solution.py:123
  109.7 1.9 collective-permute-start.3
  111.6 7.2 %collective-permute-start.2 = (f32[4,12,2]{2,1,0:T(8,128)S(1)}, f32[4,12,2]{2,1,0:T(8,128)S(1)}, u32[]{:S(2)}, u32[]{:S(2)}) collective-permute-start(f32[4,12,2]{2,1,0:T(8,128)S(1)} %get-tuple-element.44), channel_id=1, source_target_pairs={{0,1},{1,2},{2,3},{4,5},{5,6},{6,7},{8,9},{9,10},{10,11},{12,13},{... | collective-permute-start | bytes 1160 | tf_op jit(solution)/shard_map/ppermute | solution.py:16
  120.9 1.9 collective-permute-start.23
  122.8 5.1 %collective-permute-start.22 = (f32[3,18,1]{2,1,0:T(8,128)S(1)}, f32[3,18,1]{2,1,0:T(8,128)S(1)}, u32[]{:S(2)}, u32[]{:S(2)}) collective-permute-start(f32[3,18,1]{2,1,0:T(8,128)S(1)} %get-tuple-element.36), channel_id=1, source_target_pairs={{0,1},{1,2},{2,3},{4,5},{5,6},{6,7},{8,9},{9,10},{10,11},{12,13},{... | collective-permute-start | bytes 656 | tf_op jit(solution)/shard_map/ppermute | solution.py:16
  128.0 2.3 concatenate.65
  134.1 4.5 %gather_fusion.2 = f32[768]{0:T(1024)S(1)} fusion(f32[32768]{0:T(1024)S(1)} %bitcast.252, s32[1024]{0:T(1024)S(1)} %get-tuple-element.110), kind=kCustom, calls=%fused_computation.2 | custom fusion | bytes 9216 | tf_op jit(solution)/shard_map/gather | solution.py:106
  138.7 1.9 collective-permute-start.24
  140.6 6.4 %collective-permute-start.25 = (f32[1,256]{1,0:T(1,128)S(1)}, f32[1,256]{1,0:T(1,128)S(1)}, u32[]{:S(2)}, u32[]{:S(2)}) collective-permute-start(f32[1,256]{1,0:T(1,128)S(1)} %get-tuple-element.92), channel_id=1, source_target_pairs={{4,0},{8,4},{12,8},{16,12},{20,16},{24,20},{28,24},{32,28},{36,32}... | collective-permute-start | bytes 3080 | tf_op jit(solution)/shard_map/ppermute | solution.py:17
  147.8 2.4 concatenate.74
  150.3 2.2 slice_bitcast_fusion.9
  152.5 4.7 %scatter_custom_fusion.2 = f32[65536]{0:T(1024)S(1)} fusion(s32[768]{0:T(1024)S(1)} %fusion.124, f32[768]{0:T(1024)S(1)} %reshape.226, f32[]{:T(128)} %constant.4.clone.1), kind=kCustom, calls=%fused_computation.228 | custom fusion | flops 768 | bytes 262148 | tf_op jit(solution)/shard_map/scatter-add | solution.py:112
  157.2 2.0 fusion.61
  159.3 2.1 collective-permute-start.26
  161.4 6.2 %collective-permute-start.27 = (f32[2,1,4096]{2,1,0:T(1,128)S(1)}, f32[2,1,4096]{2,1,0:T(1,128)S(1)}, u32[]{:S(2)}, u32[]{:S(2)}) collective-permute-start(f32[2,1,4096]{2,1,0:T(1,128)S(1)} %get-tuple-element.66), channel_id=1, source_target_pairs={{4,0},{8,4},{12,8},{16,12},{20,16},{24,20},{28,24},{32,28},{36,32}... | collective-permute-start | bytes 98312 | tf_op jit(solution)/shard_map/ppermute | solution.py:17
  172.5 5.1 %collective-permute-start.28 = (f32[2,18,1]{2,1,0:T(8,128)S(1)}, f32[2,18,1]{2,1,0:T(8,128)S(1)}, u32[]{:S(2)}, u32[]{:S(2)}) collective-permute-start(f32[2,18,1]{2,1,0:T(8,128)S(1)} %get-tuple-element.56), channel_id=1, source_target_pairs={{0,1},{1,2},{2,3},{4,5},{5,6},{6,7},{8,9},{9,10},{10,11},{12,13},{... | collective-permute-start | bytes 440 | tf_op jit(solution)/shard_map/ppermute | solution.py:16
  177.6 6.4 %collective-permute-start.17 = (f32[4,2,4096]{2,1,0:T(2,128)}, f32[4,2,4096]{2,1,0:T(2,128)}, u32[]{:S(2)}, u32[]{:S(2)}) collective-permute-start(f32[4,2,4096]{2,1,0:T(2,128)} %get-tuple-element.68), channel_id=1, source_target_pairs={{4,0},{8,4},{12,8},{16,12},{20,16},{24,20},{28,24},{32,28},{36,32}... | collective-permute-start | bytes 393224 | tf_op jit(solution)/shard_map/ppermute | solution.py:17
  187.8 4.5 %gather_fusion.3 = f32[768]{0:T(1024)S(1)} fusion(f32[65536]{0:T(1024)S(1)} %bitcast.255, s32[1024]{0:T(1024)S(1)} %get-tuple-element.109), kind=kCustom, calls=%fused_computation.3 | custom fusion | bytes 9216 | tf_op jit(solution)/shard_map/gather | solution.py:117
  192.2 1.9 collective-permute-start.30
  194.2 6.4 %collective-permute-start.31 = (f32[1,256]{1,0:T(1,128)S(1)}, f32[1,256]{1,0:T(1,128)S(1)}, u32[]{:S(2)}, u32[]{:S(2)}) collective-permute-start(f32[1,256]{1,0:T(1,128)S(1)} %bitcast.287), channel_id=1, source_target_pairs={{4,0},{8,4},{12,8},{16,12},{20,16},{24,20},{28,24},{32,28},{36,32}... | collective-permute-start | bytes 3080 | tf_op jit(solution)/shard_map/ppermute | solution.py:17
  200.6 1.9 collective-permute-start.36
  202.6 6.4 %collective-permute-start.37 = (f32[3,1,4096]{2,1,0:T(1,128)S(1)}, f32[3,1,4096]{2,1,0:T(1,128)S(1)}, u32[]{:S(2)}, u32[]{:S(2)}) collective-permute-start(f32[3,1,4096]{2,1,0:T(1,128)S(1)} %get-tuple-element.54), channel_id=1, source_target_pairs={{4,0},{8,4},{12,8},{16,12},{20,16},{24,20},{28,24},{32,28},{36,32}... | collective-permute-start | bytes 147464 | tf_op jit(solution)/shard_map/ppermute | solution.py:17
  211.4 1.9 collective-permute-start.39
  213.3 5.1 %collective-permute-start.38 = (f32[3,18,1]{2,1,0:T(8,128)S(1)}, f32[3,18,1]{2,1,0:T(8,128)S(1)}, u32[]{:S(2)}, u32[]{:S(2)}) collective-permute-start(f32[3,18,1]{2,1,0:T(8,128)S(1)} %get-tuple-element.34), channel_id=1, source_target_pairs={{0,1},{1,2},{2,3},{4,5},{5,6},{6,7},{8,9},{9,10},{10,11},{12,13},{... | collective-permute-start | bytes 656 | tf_op jit(solution)/shard_map/ppermute | solution.py:16
  218.5 4.6 %scatter_custom_fusion.3 = f32[32768]{0:T(1024)S(1)} fusion(s32[768]{0:T(1024)S(1)} %fusion.123, f32[768]{0:T(1024)S(1)} %reshape.234, f32[]{:T(128)} %constant.4.clone.1), kind=kCustom, calls=%fused_computation.235 | custom fusion | flops 768 | bytes 131076 | tf_op jit(solution)/shard_map/scatter-add | solution.py:123
  223.8 2.6 concatenate.81
  227.7 1.9 collective-permute-start.19
  229.6 5.1 %collective-permute-start.18 = (f32[4,12,2]{2,1,0:T(8,128)S(1)}, f32[4,12,2]{2,1,0:T(8,128)S(1)}, u32[]{:S(2)}, u32[]{:S(2)}) collective-permute-start(f32[4,12,2]{2,1,0:T(8,128)S(1)} %get-tuple-element.42), channel_id=1, source_target_pairs={{0,1},{1,2},{2,3},{4,5},{5,6},{6,7},{8,9},{9,10},{10,11},{12,13},{... | collective-permute-start | bytes 1160 | tf_op jit(solution)/shard_map/ppermute | solution.py:16
  235.8 2.3 concatenate.72
  241.7 4.5 %gather_fusion.4 = f32[768]{0:T(1024)S(1)} fusion(f32[32768]{0:T(1024)S(1)} %bitcast.251, s32[1024]{0:T(1024)S(1)} %get-tuple-element.110), kind=kCustom, calls=%fused_computation.4 | custom fusion | bytes 9216 | tf_op jit(solution)/shard_map/gather | solution.py:106
  246.2 1.9 collective-permute-start.40
  248.2 6.7 %collective-permute-start.41 = (f32[1,256]{1,0:T(1,128)S(1)}, f32[1,256]{1,0:T(1,128)S(1)}, u32[]{:S(2)}, u32[]{:S(2)}) collective-permute-start(f32[1,256]{1,0:T(1,128)S(1)} %get-tuple-element.86), channel_id=1, source_target_pairs={{4,0},{8,4},{12,8},{16,12},{20,16},{24,20},{28,24},{32,28},{36,32}... | collective-permute-start | bytes 3080 | tf_op jit(solution)/shard_map/ppermute | solution.py:17
  256.7 5.3 %scatter_custom_fusion.4 = f32[65536]{0:T(1024)} fusion(s32[768]{0:T(1024)S(1)} %fusion.124, f32[768]{0:T(1024)S(1)} %reshape.242, f32[]{:T(128)} %constant.4.clone.1), kind=kCustom, calls=%fused_computation.226 | custom fusion | flops 768 | bytes 262148 | tf_op jit(solution)/shard_map/scatter-add | solution.py:112
  263.0 2.0 fusion.44
  265.0 1.9 collective-permute-start.42
  267.0 6.4 %collective-permute-start.43 = (f32[2,1,4096]{2,1,0:T(1,128)S(1)}, f32[2,1,4096]{2,1,0:T(1,128)S(1)}, u32[]{:S(2)}, u32[]{:S(2)}) collective-permute-start(f32[2,1,4096]{2,1,0:T(1,128)S(1)} %get-tuple-element.62), channel_id=1, source_target_pairs={{4,0},{8,4},{12,8},{16,12},{20,16},{24,20},{28,24},{32,28},{36,32}... | collective-permute-start | bytes 98312 | tf_op jit(solution)/shard_map/ppermute | solution.py:17
  273.5 1.9 collective-permute-start.32
  275.6 1.9 collective-permute-start.45
  277.5 7.2 %collective-permute-start.44 = (f32[2,18,1]{2,1,0:T(8,128)S(1)}, f32[2,18,1]{2,1,0:T(8,128)S(1)}, u32[]{:S(2)}, u32[]{:S(2)}) collective-permute-start(f32[2,18,1]{2,1,0:T(8,128)S(1)} %get-tuple-element.52), channel_id=1, source_target_pairs={{0,1},{1,2},{2,3},{4,5},{5,6},{6,7},{8,9},{9,10},{10,11},{12,13},{... | collective-permute-start | bytes 440 | tf_op jit(solution)/shard_map/ppermute | solution.py:16
  284.7 6.0 %collective-permute-start.33 = (f32[4,2,4096]{2,1,0:T(2,128)S(1)}, f32[4,2,4096]{2,1,0:T(2,128)S(1)}, u32[]{:S(2)}, u32[]{:S(2)}) collective-permute-start(f32[4,2,4096]{2,1,0:T(2,128)S(1)} %get-tuple-element.64), channel_id=1, source_target_pairs={{4,0},{8,4},{12,8},{16,12},{20,16},{24,20},{28,24},{32,28},{36,32}... | collective-permute-start | bytes 393224 | tf_op jit(solution)/shard_map/ppermute | solution.py:17
  295.4 4.5 %gather_fusion.5 = f32[768]{0:T(1024)S(1)} fusion(f32[65536]{0:T(1024)S(1)} %bitcast.253, s32[1024]{0:T(1024)S(1)} %get-tuple-element.109), kind=kCustom, calls=%fused_computation.5 | custom fusion | bytes 9216 | tf_op jit(solution)/shard_map/gather | solution.py:117
  299.8 1.9 collective-permute-start.46
  301.8 6.4 %collective-permute-start.47 = (f32[1,256]{1,0:T(1,128)S(1)}, f32[1,256]{1,0:T(1,128)S(1)}, u32[]{:S(2)}, u32[]{:S(2)}) collective-permute-start(f32[1,256]{1,0:T(1,128)S(1)} %bitcast.284), channel_id=1, source_target_pairs={{4,0},{8,4},{12,8},{16,12},{20,16},{24,20},{28,24},{32,28},{36,32}... | collective-permute-start | bytes 3080 | tf_op jit(solution)/shard_map/ppermute | solution.py:17
  308.5 1.9 collective-permute-start.35
  310.4 5.1 %collective-permute-start.34 = (f32[4,12,2]{2,1,0:T(8,128)S(1)}, f32[4,12,2]{2,1,0:T(8,128)S(1)}, u32[]{:S(2)}, u32[]{:S(2)}) collective-permute-start(f32[4,12,2]{2,1,0:T(8,128)S(1)} %get-tuple-element.40), channel_id=1, source_target_pairs={{0,1},{1,2},{2,3},{4,5},{5,6},{6,7},{8,9},{9,10},{10,11},{12,13},{... | collective-permute-start | bytes 1160 | tf_op jit(solution)/shard_map/ppermute | solution.py:16
  315.6 4.6 %scatter_custom_fusion.5 = f32[32768]{0:T(1024)S(1)} fusion(s32[768]{0:T(1024)S(1)} %fusion.123, f32[768]{0:T(1024)S(1)} %reshape.250, f32[]{:T(128)} %constant.4.clone.1), kind=kCustom, calls=%fused_computation.233 | custom fusion | flops 768 | bytes 131076 | tf_op jit(solution)/shard_map/scatter-add | solution.py:123
  (226 shorter events, 56.2 us)
Async XLA Ops:
  1.8 42.3 %collective-permute-start.4 = (f32[3,1,4096]{2,1,0:T(1,128)S(1)}, f32[3,1,4096]{2,1,0:T(1,128)S(1)}, u32[]{:S(2)}, u32[]{:S(2)}) collective-permute-start(f32[3,1,4096]{2,1,0:T(1,128)S(1)} %get-tuple-element.22), channel_id=1, source_target_pairs={{0,4},{4,8},{8,12},{12,16},{16,20},{20,24},{24,28},{28,32},{32,36}... | collective-permute-start | bytes 147464 | tf_op jit(solution)/shard_map/ppermute | solution.py:16
  4.9 39.2 %collective-permute-start.5 = (f32[3,1,4096]{2,1,0:T(1,128)S(1)}, f32[3,1,4096]{2,1,0:T(1,128)S(1)}, u32[]{:S(2)}, u32[]{:S(2)}) collective-permute-start(f32[3,1,4096]{2,1,0:T(1,128)S(1)} %get-tuple-element.23), channel_id=1, source_target_pairs={{4,0},{8,4},{12,8},{16,12},{20,16},{24,20},{28,24},{32,28},{36,32}... | collective-permute-start | bytes 147464 | tf_op jit(solution)/shard_map/ppermute | solution.py:17
  16.4 18.5 %copy-start.26 = (f32[2,8,4096]{2,1,0:T(8,128)S(1)}, f32[2,8,4096]{2,1,0:T(8,128)}, u32[]{:S(2)}) copy-start(f32[2,8,4096]{2,1,0:T(8,128)} %param.10) | copy-start | bytes 786436
  16.5 18.5 %copy-start.17 = (f32[3,8,4096]{2,1,0:T(8,128)S(1)}, f32[3,8,4096]{2,1,0:T(8,128)}, u32[]{:S(2)}) copy-start(f32[3,8,4096]{2,1,0:T(8,128)} %param.9) | copy-start | bytes 1179652
  26.6 11.1 %collective-permute-start.8 = (f32[1,256]{1,0:T(1,128)S(1)}, f32[1,256]{1,0:T(1,128)S(1)}, u32[]{:S(2)}, u32[]{:S(2)}) collective-permute-start(f32[1,256]{1,0:T(1,128)S(1)} %get-tuple-element.97), channel_id=1, source_target_pairs={{0,4},{4,8},{8,12},{12,16},{16,20},{20,24},{24,28},{28,32},{32,36}... | collective-permute-start | bytes 3080 | tf_op jit(solution)/shard_map/ppermute | solution.py:16
  28.6 15.5 %collective-permute-start.9 = (f32[1,256]{1,0:T(1,128)S(1)}, f32[1,256]{1,0:T(1,128)S(1)}, u32[]{:S(2)}, u32[]{:S(2)}) collective-permute-start(f32[1,256]{1,0:T(1,128)S(1)} %get-tuple-element.98), channel_id=1, source_target_pairs={{4,0},{8,4},{12,8},{16,12},{20,16},{24,20},{28,24},{32,28},{36,32}... | collective-permute-start | bytes 3080 | tf_op jit(solution)/shard_map/ppermute | solution.py:17
  35.0 9.2 %slice-start = ((f32[5,16,4096]{2,1,0:T(8,128)}), f32[3,16,4096]{2,1,0:T(8,128)S(1)}, s32[]{:S(2)}) async-start(f32[5,16,4096]{2,1,0:T(8,128)} %param.11), calls=%async_computation | async-start | bytes 1572864 | tf_op jit(solution)/shard_map/slice | solution.py:71
  35.8 72.5 %collective-permute-start = (f32[4,2,4096]{2,1,0:T(2,128)}, f32[4,2,4096]{2,1,0:T(2,128)}, u32[]{:S(2)}, u32[]{:S(2)}) collective-permute-start(f32[4,2,4096]{2,1,0:T(2,128)} %get-tuple-element.71), channel_id=1, source_target_pairs={{0,4},{4,8},{8,12},{12,16},{16,20},{20,24},{24,28},{28,32},{32,36}... | collective-permute-start | bytes 393224 | tf_op jit(solution)/shard_map/ppermute | solution.py:16
  37.7 70.6 %collective-permute-start.1 = (f32[4,2,4096]{2,1,0:T(2,128)}, f32[4,2,4096]{2,1,0:T(2,128)}, u32[]{:S(2)}, u32[]{:S(2)}) collective-permute-start(f32[4,2,4096]{2,1,0:T(2,128)} %get-tuple-element.72), channel_id=1, source_target_pairs={{4,0},{8,4},{12,8},{16,12},{20,16},{24,20},{28,24},{32,28},{36,32}... | collective-permute-start | bytes 393224 | tf_op jit(solution)/shard_map/ppermute | solution.py:17
  44.4 13.0 %collective-permute-start.7 = (f32[3,18,1]{2,1,0:T(8,128)S(1)}, f32[3,18,1]{2,1,0:T(8,128)S(1)}, u32[]{:S(2)}, u32[]{:S(2)}) collective-permute-start(f32[3,18,1]{2,1,0:T(8,128)S(1)} %get-tuple-element.37), channel_id=1, source_target_pairs={{1,0},{2,1},{3,2},{5,4},{6,5},{7,6},{9,8},{10,9},{11,10},{13,12},{... | collective-permute-start | bytes 656 | tf_op jit(solution)/shard_map/ppermute | solution.py:17
  48.4 9.0 %collective-permute-start.6 = (f32[3,18,1]{2,1,0:T(8,128)S(1)}, f32[3,18,1]{2,1,0:T(8,128)S(1)}, u32[]{:S(2)}, u32[]{:S(2)}) collective-permute-start(f32[3,18,1]{2,1,0:T(8,128)S(1)} %get-tuple-element.38), channel_id=1, source_target_pairs={{0,1},{1,2},{2,3},{4,5},{5,6},{6,7},{8,9},{9,10},{10,11},{12,13},{... | collective-permute-start | bytes 656 | tf_op jit(solution)/shard_map/ppermute | solution.py:16
  61.2 8.3 %collective-permute-start.10 = (f32[2,1,4096]{2,1,0:T(1,128)S(1)}, f32[2,1,4096]{2,1,0:T(1,128)S(1)}, u32[]{:S(2)}, u32[]{:S(2)}) collective-permute-start(f32[2,1,4096]{2,1,0:T(1,128)S(1)} %get-tuple-element.69), channel_id=1, source_target_pairs={{0,4},{4,8},{8,12},{12,16},{16,20},{20,24},{24,28},{28,32},{32,36}... | collective-permute-start | bytes 98312 | tf_op jit(solution)/shard_map/ppermute | solution.py:16
  63.1 7.4 %collective-permute-start.11 = (f32[2,1,4096]{2,1,0:T(1,128)S(1)}, f32[2,1,4096]{2,1,0:T(1,128)S(1)}, u32[]{:S(2)}, u32[]{:S(2)}) collective-permute-start(f32[2,1,4096]{2,1,0:T(1,128)S(1)} %get-tuple-element.70), channel_id=1, source_target_pairs={{4,0},{8,4},{12,8},{16,12},{20,16},{24,20},{28,24},{32,28},{36,32}... | collective-permute-start | bytes 98312 | tf_op jit(solution)/shard_map/ppermute | solution.py:17
  70.7 7.1 %collective-permute-start.13 = (f32[2,18,1]{2,1,0:T(8,128)S(1)}, f32[2,18,1]{2,1,0:T(8,128)S(1)}, u32[]{:S(2)}, u32[]{:S(2)}) collective-permute-start(f32[2,18,1]{2,1,0:T(8,128)S(1)} %get-tuple-element.59), channel_id=1, source_target_pairs={{1,0},{2,1},{3,2},{5,4},{6,5},{7,6},{9,8},{10,9},{11,10},{13,12},{... | collective-permute-start | bytes 440 | tf_op jit(solution)/shard_map/ppermute | solution.py:17
  72.6 6.1 %collective-permute-start.12 = (f32[2,18,1]{2,1,0:T(8,128)S(1)}, f32[2,18,1]{2,1,0:T(8,128)S(1)}, u32[]{:S(2)}, u32[]{:S(2)}) collective-permute-start(f32[2,18,1]{2,1,0:T(8,128)S(1)} %get-tuple-element.60), channel_id=1, source_target_pairs={{0,1},{1,2},{2,3},{4,5},{5,6},{6,7},{8,9},{9,10},{10,11},{12,13},{... | collective-permute-start | bytes 440 | tf_op jit(solution)/shard_map/ppermute | solution.py:16
  81.7 37.1 %copy-start.6 = (f32[16,4096]{1,0:T(8,128)}, f32[16,4096]{1,0:T(8,128)S(1)}, u32[]{:S(2)}) copy-start(f32[16,4096]{1,0:T(8,128)S(1)} %fusion.65) | copy-start | bytes 786436
  82.0 36.8 %copy-start.10 = (f32[16,4096]{1,0:T(8,128)}, f32[16,4096]{1,0:T(8,128)S(1)}, u32[]{:S(2)}) copy-start(f32[16,4096]{1,0:T(8,128)S(1)} %get-tuple-element.6) | copy-start | bytes 786436
  86.6 10.6 %collective-permute-start.14 = (f32[1,256]{1,0:T(1,128)S(1)}, f32[1,256]{1,0:T(1,128)S(1)}, u32[]{:S(2)}, u32[]{:S(2)}) collective-permute-start(f32[1,256]{1,0:T(1,128)S(1)} %bitcast.288), channel_id=1, source_target_pairs={{0,4},{4,8},{8,12},{12,16},{16,20},{20,24},{24,28},{28,32},{32,36}... | collective-permute-start | bytes 3080 | tf_op jit(solution)/shard_map/ppermute | solution.py:16
  88.5 15.1 %collective-permute-start.15 = (f32[1,256]{1,0:T(1,128)S(1)}, f32[1,256]{1,0:T(1,128)S(1)}, u32[]{:S(2)}, u32[]{:S(2)}) collective-permute-start(f32[1,256]{1,0:T(1,128)S(1)} %bitcast.286), channel_id=1, source_target_pairs={{4,0},{8,4},{12,8},{16,12},{20,16},{24,20},{28,24},{32,28},{36,32}... | collective-permute-start | bytes 3080 | tf_op jit(solution)/shard_map/ppermute | solution.py:17
  95.3 23.5 %collective-permute-start.20 = (f32[3,1,4096]{2,1,0:T(1,128)S(1)}, f32[3,1,4096]{2,1,0:T(1,128)S(1)}, u32[]{:S(2)}, u32[]{:S(2)}) collective-permute-start(f32[3,1,4096]{2,1,0:T(1,128)S(1)} %get-tuple-element.57), channel_id=1, source_target_pairs={{0,4},{4,8},{8,12},{12,16},{16,20},{20,24},{24,28},{28,32},{32,36}... | collective-permute-start | bytes 147464 | tf_op jit(solution)/shard_map/ppermute | solution.py:16
  97.2 21.6 %collective-permute-start.21 = (f32[3,1,4096]{2,1,0:T(1,128)S(1)}, f32[3,1,4096]{2,1,0:T(1,128)}, u32[]{:S(2)}, u32[]{:S(2)}) collective-permute-start(f32[3,1,4096]{2,1,0:T(1,128)S(1)} %get-tuple-element.58), channel_id=1, source_target_pairs={{4,0},{8,4},{12,8},{16,12},{20,16},{24,20},{28,24},{32,28},{36,32}... | collective-permute-start | bytes 147464 | tf_op jit(solution)/shard_map/ppermute | solution.py:17
  109.6 9.2 %copy-start.4 = (f32[4,12,4096]{2,1,0:T(8,128)}, f32[4,12,4096]{2,1,0:T(8,128)S(1)}, u32[]{:S(2)}) copy-start(f32[4,12,4096]{2,1,0:T(8,128)S(1)} %fusion.1) | copy-start | bytes 2359300
  109.7 18.3 %collective-permute-start.3 = (f32[4,12,2]{2,1,0:T(8,128)S(1)}, f32[4,12,2]{2,1,0:T(8,128)S(1)}, u32[]{:S(2)}, u32[]{:S(2)}) collective-permute-start(f32[4,12,2]{2,1,0:T(8,128)S(1)} %get-tuple-element.43), channel_id=1, source_target_pairs={{1,0},{2,1},{3,2},{5,4},{6,5},{7,6},{9,8},{10,9},{11,10},{13,12},{... | collective-permute-start | bytes 1160 | tf_op jit(solution)/shard_map/ppermute | solution.py:17
  111.6 16.4 %collective-permute-start.2 = (f32[4,12,2]{2,1,0:T(8,128)S(1)}, f32[4,12,2]{2,1,0:T(8,128)S(1)}, u32[]{:S(2)}, u32[]{:S(2)}) collective-permute-start(f32[4,12,2]{2,1,0:T(8,128)S(1)} %get-tuple-element.44), channel_id=1, source_target_pairs={{0,1},{1,2},{2,3},{4,5},{5,6},{6,7},{8,9},{9,10},{10,11},{12,13},{... | collective-permute-start | bytes 1160 | tf_op jit(solution)/shard_map/ppermute | solution.py:16
  120.9 26.9 %collective-permute-start.23 = (f32[3,18,1]{2,1,0:T(8,128)S(1)}, f32[3,18,1]{2,1,0:T(8,128)S(1)}, u32[]{:S(2)}, u32[]{:S(2)}) collective-permute-start(f32[3,18,1]{2,1,0:T(8,128)S(1)} %get-tuple-element.35), channel_id=1, source_target_pairs={{1,0},{2,1},{3,2},{5,4},{6,5},{7,6},{9,8},{10,9},{11,10},{13,12},{... | collective-permute-start | bytes 656 | tf_op jit(solution)/shard_map/ppermute | solution.py:17
  122.8 25.0 %collective-permute-start.22 = (f32[3,18,1]{2,1,0:T(8,128)S(1)}, f32[3,18,1]{2,1,0:T(8,128)S(1)}, u32[]{:S(2)}, u32[]{:S(2)}) collective-permute-start(f32[3,18,1]{2,1,0:T(8,128)S(1)} %get-tuple-element.36), channel_id=1, source_target_pairs={{0,1},{1,2},{2,3},{4,5},{5,6},{6,7},{8,9},{9,10},{10,11},{12,13},{... | collective-permute-start | bytes 656 | tf_op jit(solution)/shard_map/ppermute | solution.py:16
  134.1 12.9 %copy-start.13 = (f32[8,4096]{1,0:T(8,128)}, f32[8,4096]{1,0:T(8,128)S(1)}, u32[]{:S(2)}) copy-start(f32[8,4096]{1,0:T(8,128)S(1)} %get-tuple-element.79) | copy-start | bytes 393220
  134.1 12.9 %copy-start.18 = (f32[1,8,4096]{2,1,0:T(8,128)}, f32[1,8,4096]{2,1,0:T(8,128)S(1)}, u32[]{:S(2)}) copy-start(f32[1,8,4096]{2,1,0:T(8,128)S(1)} %get-tuple-element.80) | copy-start | bytes 393220
  134.1 12.9 %copy-start.20 = (f32[1,8,4096]{2,1,0:T(8,128)}, f32[1,8,4096]{2,1,0:T(8,128)S(1)}, u32[]{:S(2)}) copy-start(f32[1,8,4096]{2,1,0:T(8,128)S(1)} %get-tuple-element.81) | copy-start | bytes 393220
  138.7 13.8 %collective-permute-start.24 = (f32[1,256]{1,0:T(1,128)S(1)}, f32[1,256]{1,0:T(1,128)S(1)}, u32[]{:S(2)}, u32[]{:S(2)}) collective-permute-start(f32[1,256]{1,0:T(1,128)S(1)} %get-tuple-element.91), channel_id=1, source_target_pairs={{0,4},{4,8},{8,12},{12,16},{16,20},{20,24},{24,28},{28,32},{32,36}... | collective-permute-start | bytes 3080 | tf_op jit(solution)/shard_map/ppermute | solution.py:16
  140.6 11.9 %collective-permute-start.25 = (f32[1,256]{1,0:T(1,128)S(1)}, f32[1,256]{1,0:T(1,128)S(1)}, u32[]{:S(2)}, u32[]{:S(2)}) collective-permute-start(f32[1,256]{1,0:T(1,128)S(1)} %get-tuple-element.92), channel_id=1, source_target_pairs={{4,0},{8,4},{12,8},{16,12},{20,16},{24,20},{28,24},{32,28},{36,32}... | collective-permute-start | bytes 3080 | tf_op jit(solution)/shard_map/ppermute | solution.py:17
  157.2 10.4 %copy-start.24 = (f32[4,8,4096]{2,1,0:T(8,128)S(1)}, f32[4,8,4096]{2,1,0:T(8,128)}, u32[]{:S(2)}) copy-start(f32[4,8,4096]{2,1,0:T(8,128)} %pad_maximum_fusion.7) | copy-start | bytes 1572868
  159.3 11.0 %collective-permute-start.26 = (f32[2,1,4096]{2,1,0:T(1,128)S(1)}, f32[2,1,4096]{2,1,0:T(1,128)S(1)}, u32[]{:S(2)}, u32[]{:S(2)}) collective-permute-start(f32[2,1,4096]{2,1,0:T(1,128)S(1)} %get-tuple-element.65), channel_id=1, source_target_pairs={{0,4},{4,8},{8,12},{12,16},{16,20},{20,24},{24,28},{28,32},{32,36}... | collective-permute-start | bytes 98312 | tf_op jit(solution)/shard_map/ppermute | solution.py:16
  161.4 8.9 %collective-permute-start.27 = (f32[2,1,4096]{2,1,0:T(1,128)S(1)}, f32[2,1,4096]{2,1,0:T(1,128)S(1)}, u32[]{:S(2)}, u32[]{:S(2)}) collective-permute-start(f32[2,1,4096]{2,1,0:T(1,128)S(1)} %get-tuple-element.66), channel_id=1, source_target_pairs={{4,0},{8,4},{12,8},{16,12},{20,16},{24,20},{28,24},{32,28},{36,32}... | collective-permute-start | bytes 98312 | tf_op jit(solution)/shard_map/ppermute | solution.py:17
  168.4 58.0 %collective-permute-start.16 = (f32[4,2,4096]{2,1,0:T(2,128)}, f32[4,2,4096]{2,1,0:T(2,128)S(1)}, u32[]{:S(2)}, u32[]{:S(2)}) collective-permute-start(f32[4,2,4096]{2,1,0:T(2,128)} %get-tuple-element.67), channel_id=1, source_target_pairs={{0,4},{4,8},{8,12},{12,16},{16,20},{20,24},{24,28},{28,32},{32,36}... | collective-permute-start | bytes 393224 | tf_op jit(solution)/shard_map/ppermute | solution.py:16
  170.6 13.5 %collective-permute-start.29 = (f32[2,18,1]{2,1,0:T(8,128)S(1)}, f32[2,18,1]{2,1,0:T(8,128)S(1)}, u32[]{:S(2)}, u32[]{:S(2)}) collective-permute-start(f32[2,18,1]{2,1,0:T(8,128)S(1)} %get-tuple-element.55), channel_id=1, source_target_pairs={{1,0},{2,1},{3,2},{5,4},{6,5},{7,6},{9,8},{10,9},{11,10},{13,12},{... | collective-permute-start | bytes 440 | tf_op jit(solution)/shard_map/ppermute | solution.py:17
  172.5 11.5 %collective-permute-start.28 = (f32[2,18,1]{2,1,0:T(8,128)S(1)}, f32[2,18,1]{2,1,0:T(8,128)S(1)}, u32[]{:S(2)}, u32[]{:S(2)}) collective-permute-start(f32[2,18,1]{2,1,0:T(8,128)S(1)} %get-tuple-element.56), channel_id=1, source_target_pairs={{0,1},{1,2},{2,3},{4,5},{5,6},{6,7},{8,9},{9,10},{10,11},{12,13},{... | collective-permute-start | bytes 440 | tf_op jit(solution)/shard_map/ppermute | solution.py:16
  177.6 48.8 %collective-permute-start.17 = (f32[4,2,4096]{2,1,0:T(2,128)}, f32[4,2,4096]{2,1,0:T(2,128)}, u32[]{:S(2)}, u32[]{:S(2)}) collective-permute-start(f32[4,2,4096]{2,1,0:T(2,128)} %get-tuple-element.68), channel_id=1, source_target_pairs={{4,0},{8,4},{12,8},{16,12},{20,16},{24,20},{28,24},{32,28},{36,32}... | collective-permute-start | bytes 393224 | tf_op jit(solution)/shard_map/ppermute | solution.py:17
  187.7 22.4 %copy-start.8 = (f32[16,4096]{1,0:T(8,128)}, f32[16,4096]{1,0:T(8,128)S(1)}, u32[]{:S(2)}) copy-start(f32[16,4096]{1,0:T(8,128)S(1)} %get-tuple-element.10) | copy-start | bytes 786436
  192.2 10.3 %collective-permute-start.30 = (f32[1,256]{1,0:T(1,128)S(1)}, f32[1,256]{1,0:T(1,128)S(1)}, u32[]{:S(2)}, u32[]{:S(2)}) collective-permute-start(f32[1,256]{1,0:T(1,128)S(1)} %bitcast.289), channel_id=1, source_target_pairs={{0,4},{4,8},{8,12},{12,16},{16,20},{20,24},{24,28},{28,32},{32,36}... | collective-permute-start | bytes 3080 | tf_op jit(solution)/shard_map/ppermute | solution.py:16
  194.2 14.8 %collective-permute-start.31 = (f32[1,256]{1,0:T(1,128)S(1)}, f32[1,256]{1,0:T(1,128)S(1)}, u32[]{:S(2)}, u32[]{:S(2)}) collective-permute-start(f32[1,256]{1,0:T(1,128)S(1)} %bitcast.287), channel_id=1, source_target_pairs={{4,0},{8,4},{12,8},{16,12},{20,16},{24,20},{28,24},{32,28},{36,32}... | collective-permute-start | bytes 3080 | tf_op jit(solution)/shard_map/ppermute | solution.py:17
  200.6 8.3 %collective-permute-start.36 = (f32[3,1,4096]{2,1,0:T(1,128)S(1)}, f32[3,1,4096]{2,1,0:T(1,128)S(1)}, u32[]{:S(2)}, u32[]{:S(2)}) collective-permute-start(f32[3,1,4096]{2,1,0:T(1,128)S(1)} %get-tuple-element.53), channel_id=1, source_target_pairs={{0,4},{4,8},{8,12},{12,16},{16,20},{20,24},{24,28},{28,32},{32,36}... | collective-permute-start | bytes 147464 | tf_op jit(solution)/shard_map/ppermute | solution.py:16
  202.6 7.5 %collective-permute-start.37 = (f32[3,1,4096]{2,1,0:T(1,128)S(1)}, f32[3,1,4096]{2,1,0:T(1,128)S(1)}, u32[]{:S(2)}, u32[]{:S(2)}) collective-permute-start(f32[3,1,4096]{2,1,0:T(1,128)S(1)} %get-tuple-element.54), channel_id=1, source_target_pairs={{4,0},{8,4},{12,8},{16,12},{20,16},{24,20},{28,24},{32,28},{36,32}... | collective-permute-start | bytes 147464 | tf_op jit(solution)/shard_map/ppermute | solution.py:17
  211.4 12.4 %collective-permute-start.39 = (f32[3,18,1]{2,1,0:T(8,128)S(1)}, f32[3,18,1]{2,1,0:T(8,128)S(1)}, u32[]{:S(2)}, u32[]{:S(2)}) collective-permute-start(f32[3,18,1]{2,1,0:T(8,128)S(1)} %get-tuple-element.33), channel_id=1, source_target_pairs={{1,0},{2,1},{3,2},{5,4},{6,5},{7,6},{9,8},{10,9},{11,10},{13,12},{... | collective-permute-start | bytes 656 | tf_op jit(solution)/shard_map/ppermute | solution.py:17
  213.3 10.5 %collective-permute-start.38 = (f32[3,18,1]{2,1,0:T(8,128)S(1)}, f32[3,18,1]{2,1,0:T(8,128)S(1)}, u32[]{:S(2)}, u32[]{:S(2)}) collective-permute-start(f32[3,18,1]{2,1,0:T(8,128)S(1)} %get-tuple-element.34), channel_id=1, source_target_pairs={{0,1},{1,2},{2,3},{4,5},{5,6},{6,7},{8,9},{9,10},{10,11},{12,13},{... | collective-permute-start | bytes 656 | tf_op jit(solution)/shard_map/ppermute | solution.py:16
  227.7 8.1 %collective-permute-start.19 = (f32[4,12,2]{2,1,0:T(8,128)S(1)}, f32[4,12,2]{2,1,0:T(8,128)S(1)}, u32[]{:S(2)}, u32[]{:S(2)}) collective-permute-start(f32[4,12,2]{2,1,0:T(8,128)S(1)} %get-tuple-element.41), channel_id=1, source_target_pairs={{1,0},{2,1},{3,2},{5,4},{6,5},{7,6},{9,8},{10,9},{11,10},{13,12},{... | collective-permute-start | bytes 1160 | tf_op jit(solution)/shard_map/ppermute | solution.py:17
  229.6 6.2 %collective-permute-start.18 = (f32[4,12,2]{2,1,0:T(8,128)S(1)}, f32[4,12,2]{2,1,0:T(8,128)S(1)}, u32[]{:S(2)}, u32[]{:S(2)}) collective-permute-start(f32[4,12,2]{2,1,0:T(8,128)S(1)} %get-tuple-element.42), channel_id=1, source_target_pairs={{0,1},{1,2},{2,3},{4,5},{5,6},{6,7},{8,9},{9,10},{10,11},{12,13},{... | collective-permute-start | bytes 1160 | tf_op jit(solution)/shard_map/ppermute | solution.py:16
  241.7 13.2 %copy-start.15 = (f32[8,4096]{1,0:T(8,128)}, f32[8,4096]{1,0:T(8,128)S(1)}, u32[]{:S(2)}) copy-start(f32[8,4096]{1,0:T(8,128)S(1)} %get-tuple-element.76) | copy-start | bytes 393220
  246.2 10.4 %collective-permute-start.40 = (f32[1,256]{1,0:T(1,128)S(1)}, f32[1,256]{1,0:T(1,128)S(1)}, u32[]{:S(2)}, u32[]{:S(2)}) collective-permute-start(f32[1,256]{1,0:T(1,128)S(1)} %get-tuple-element.85), channel_id=1, source_target_pairs={{0,4},{4,8},{8,12},{12,16},{16,20},{20,24},{24,28},{28,32},{32,36}... | collective-permute-start | bytes 3080 | tf_op jit(solution)/shard_map/ppermute | solution.py:16
  248.2 8.5 %collective-permute-start.41 = (f32[1,256]{1,0:T(1,128)S(1)}, f32[1,256]{1,0:T(1,128)S(1)}, u32[]{:S(2)}, u32[]{:S(2)}) collective-permute-start(f32[1,256]{1,0:T(1,128)S(1)} %get-tuple-element.86), channel_id=1, source_target_pairs={{4,0},{8,4},{12,8},{16,12},{20,16},{24,20},{28,24},{32,28},{36,32}... | collective-permute-start | bytes 3080 | tf_op jit(solution)/shard_map/ppermute | solution.py:17
  263.0 10.4 %copy-start.25 = (f32[4,8,4096]{2,1,0:T(8,128)S(1)}, f32[4,8,4096]{2,1,0:T(8,128)}, u32[]{:S(2)}) copy-start(f32[4,8,4096]{2,1,0:T(8,128)} %pad_maximum_fusion.6) | copy-start | bytes 1572868
  265.0 10.3 %collective-permute-start.42 = (f32[2,1,4096]{2,1,0:T(1,128)S(1)}, f32[2,1,4096]{2,1,0:T(1,128)S(1)}, u32[]{:S(2)}, u32[]{:S(2)}) collective-permute-start(f32[2,1,4096]{2,1,0:T(1,128)S(1)} %get-tuple-element.61), channel_id=1, source_target_pairs={{0,4},{4,8},{8,12},{12,16},{16,20},{20,24},{24,28},{28,32},{32,36}... | collective-permute-start | bytes 98312 | tf_op jit(solution)/shard_map/ppermute | solution.py:16
  267.0 8.4 %collective-permute-start.43 = (f32[2,1,4096]{2,1,0:T(1,128)S(1)}, f32[2,1,4096]{2,1,0:T(1,128)S(1)}, u32[]{:S(2)}, u32[]{:S(2)}) collective-permute-start(f32[2,1,4096]{2,1,0:T(1,128)S(1)} %get-tuple-element.62), channel_id=1, source_target_pairs={{4,0},{8,4},{12,8},{16,12},{20,16},{24,20},{28,24},{32,28},{36,32}... | collective-permute-start | bytes 98312 | tf_op jit(solution)/shard_map/ppermute | solution.py:17
  273.5 34.7 %collective-permute-start.32 = (f32[4,2,4096]{2,1,0:T(2,128)S(1)}, f32[4,2,4096]{2,1,0:T(2,128)S(1)}, u32[]{:S(2)}, u32[]{:S(2)}) collective-permute-start(f32[4,2,4096]{2,1,0:T(2,128)S(1)} %get-tuple-element.63), channel_id=1, source_target_pairs={{0,4},{4,8},{8,12},{12,16},{16,20},{20,24},{24,28},{28,32},{32,36}... | collective-permute-start | bytes 393224 | tf_op jit(solution)/shard_map/ppermute | solution.py:16
  275.6 15.1 %collective-permute-start.45 = (f32[2,18,1]{2,1,0:T(8,128)S(1)}, f32[2,18,1]{2,1,0:T(8,128)S(1)}, u32[]{:S(2)}, u32[]{:S(2)}) collective-permute-start(f32[2,18,1]{2,1,0:T(8,128)S(1)} %get-tuple-element.51), channel_id=1, source_target_pairs={{1,0},{2,1},{3,2},{5,4},{6,5},{7,6},{9,8},{10,9},{11,10},{13,12},{... | collective-permute-start | bytes 440 | tf_op jit(solution)/shard_map/ppermute | solution.py:17
  277.5 13.2 %collective-permute-start.44 = (f32[2,18,1]{2,1,0:T(8,128)S(1)}, f32[2,18,1]{2,1,0:T(8,128)S(1)}, u32[]{:S(2)}, u32[]{:S(2)}) collective-permute-start(f32[2,18,1]{2,1,0:T(8,128)S(1)} %get-tuple-element.52), channel_id=1, source_target_pairs={{0,1},{1,2},{2,3},{4,5},{5,6},{6,7},{8,9},{9,10},{10,11},{12,13},{... | collective-permute-start | bytes 440 | tf_op jit(solution)/shard_map/ppermute | solution.py:16
  284.7 23.5 %collective-permute-start.33 = (f32[4,2,4096]{2,1,0:T(2,128)S(1)}, f32[4,2,4096]{2,1,0:T(2,128)S(1)}, u32[]{:S(2)}, u32[]{:S(2)}) collective-permute-start(f32[4,2,4096]{2,1,0:T(2,128)S(1)} %get-tuple-element.64), channel_id=1, source_target_pairs={{4,0},{8,4},{12,8},{16,12},{20,16},{24,20},{28,24},{32,28},{36,32}... | collective-permute-start | bytes 393224 | tf_op jit(solution)/shard_map/ppermute | solution.py:17
  295.4 12.8 %copy-start.16 = (f32[8,4096]{1,0:T(8,128)S(1)}, f32[8,4096]{1,0:T(8,128)}, u32[]{:S(2)}) copy-start(f32[8,4096]{1,0:T(8,128)} %copy-done.15) | copy-start | bytes 393220
  295.4 12.8 %copy-start.22 = (f32[1,8,4096]{2,1,0:T(8,128)S(1)}, f32[1,8,4096]{2,1,0:T(8,128)}, u32[]{:S(2)}) copy-start(f32[1,8,4096]{2,1,0:T(8,128)} %get-tuple-element.77) | copy-start | bytes 393220
  295.4 12.8 %copy-start.23 = (f32[1,8,4096]{2,1,0:T(8,128)S(1)}, f32[1,8,4096]{2,1,0:T(8,128)}, u32[]{:S(2)}) copy-start(f32[1,8,4096]{2,1,0:T(8,128)} %get-tuple-element.78) | copy-start | bytes 393220
  299.8 15.7 %collective-permute-start.46 = (f32[1,256]{1,0:T(1,128)S(1)}, f32[1,256]{1,0:T(1,128)S(1)}, u32[]{:S(2)}, u32[]{:S(2)}) collective-permute-start(f32[1,256]{1,0:T(1,128)S(1)} %bitcast.285), channel_id=1, source_target_pairs={{0,4},{4,8},{8,12},{12,16},{16,20},{20,24},{24,28},{28,32},{32,36}... | collective-permute-start | bytes 3080 | tf_op jit(solution)/shard_map/ppermute | solution.py:16
  301.8 13.8 %collective-permute-start.47 = (f32[1,256]{1,0:T(1,128)S(1)}, f32[1,256]{1,0:T(1,128)S(1)}, u32[]{:S(2)}, u32[]{:S(2)}) collective-permute-start(f32[1,256]{1,0:T(1,128)S(1)} %bitcast.284), channel_id=1, source_target_pairs={{4,0},{8,4},{12,8},{16,12},{20,16},{24,20},{28,24},{32,28},{36,32}... | collective-permute-start | bytes 3080 | tf_op jit(solution)/shard_map/ppermute | solution.py:17
  308.5 11.8 %collective-permute-start.35 = (f32[4,12,2]{2,1,0:T(8,128)S(1)}, f32[4,12,2]{2,1,0:T(8,128)S(1)}, u32[]{:S(2)}, u32[]{:S(2)}) collective-permute-start(f32[4,12,2]{2,1,0:T(8,128)S(1)} %get-tuple-element.39), channel_id=1, source_target_pairs={{1,0},{2,1},{3,2},{5,4},{6,5},{7,6},{9,8},{10,9},{11,10},{13,12},{... | collective-permute-start | bytes 1160 | tf_op jit(solution)/shard_map/ppermute | solution.py:17
  310.4 9.9 %collective-permute-start.34 = (f32[4,12,2]{2,1,0:T(8,128)S(1)}, f32[4,12,2]{2,1,0:T(8,128)S(1)}, u32[]{:S(2)}, u32[]{:S(2)}) collective-permute-start(f32[4,12,2]{2,1,0:T(8,128)S(1)} %get-tuple-element.40), channel_id=1, source_target_pairs={{0,1},{1,2},{2,3},{4,5},{5,6},{6,7},{8,9},{9,10},{10,11},{12,13},{... | collective-permute-start | bytes 1160 | tf_op jit(solution)/shard_map/ppermute | solution.py:16
  (19 other events, 43.0 us)
where the time goes:
time: 325 us; the launch traced here: 323 us
  starting transfers between devices  196 us (60%)
  local copies, waits for them, and re-layouts  65.4 us (20%)
  other arithmetic  56.7 us (17%)
    ppermute x24, starting transfers between devices, padded(): after = lax.ppermute(initial, axis, down)  116 us
    ppermute x24, starting transfers between devices, padded(): before = lax.ppermute(last, axis, up)  79.6 us
    concatenate x9, local copies, waits for them, and re-layouts, padded(): array = jnp.concatenate([before, array, after], axis=dim)  14.7 us
    scatter-add x3, other arithmetic, on_device(): loading = jnp.zeros((steel_rows * steel_columns,), jnp.float32).at[steel_...  14.6 us
    scatter-add x3, other arithmetic, on_device(): feeding = jnp.zeros((water_rows * water_columns,), jnp.float32).at[water_...  13.9 us
    gather x3, local copies, waits for them, and re-layouts, on_device(): water_state[0].reshape(-1)[water_flat].reshape(factor.shape) * factor  13.4 us
    gather x3, local copies, waits for them, and re-layouts, on_device(): traction = steel_state[3].reshape(-1)[steel_flat].reshape(factor.shape)  13.4 us
    unnamed x79, local copies, waits for them, and re-layouts  8.56 us
  transfers between devices with their start and end apart: 48, of which 3 were waited for; matrix products, arithmetic and copies ran while one was open for 27% of the time, Pallas kernels for 0%

commit v1 on v0

v1 whole, which is shorter than its diff:
```python
import functools

import jax
import jax.numpy as jnp
from jax import lax
from jax.experimental import pallas as pl
from jax.experimental.pallas import tpu as pltpu
from jax.sharding import PartitionSpec as P

MESH = pl.DeviceIdType.MESH
STEPS = 3
LANES = 128
F32 = jnp.float32
BF16 = jnp.bfloat16


def split_two(x):
    first = x.astype(BF16)
    return first, (x - first.astype(F32)).astype(BF16)


class Columns:
    def __init__(self, get, left, right, count, shape):
        self.get, self.left, self.right, self.count = get, left, right, count
        lane = lax.broadcasted_iota(jnp.int32, shape, 1)
        self.is_first, self.is_last = lane == 0, lane == LANES - 1
        self.before, self.after = {}, {}

    def tile(self, h):
        return self.left() if h < 0 else self.right() if h == self.count else self.get(h)

    def rolled(self, h, cache, shift):
        if h not in cache:
            cache[h] = pltpu.roll(self.tile(h), shift, 1)
        return cache[h]

    def __call__(self, h):
        previous = jnp.where(
            self.is_first, self.rolled(h - 1, self.before, 1), self.rolled(h, self.before, 1)
        )
        following = jnp.where(
            self.is_last,
            self.rolled(h + 1, self.after, LANES - 1),
            self.rolled(h, self.after, LANES - 1),
        )
        return following - previous


def row_difference(tile, above, below, is_top, is_bottom):
    rows = tile.shape[0]
    previous = jnp.where(is_top, above, pltpu.roll(tile, 1, 0))
    following = jnp.where(is_bottom, below, pltpu.roll(tile, rows - 1, 0))
    return following - previous


def kernel(
    dims,
    coupling,
    counts,
    water_cell,
    stencil_code,
    steel_cell,
    water_in,
    water_coef_in,
    steel_in,
    steel_coef_in,
    water_out,
    steel_out,
    W,
    WC,
    S,
    SC,
    RW,
    RS,
    LW,
    LS,
    FAC,
    LOAD,
    lists_out,
    lists_in,
    stress_rows_out,
    stress_rows_in,
    speed_rows_out,
    speed_rows_in,
    p_rows_out,
    p_rows_in,
    vx_rows_out,
    vx_rows_in,
    stress_cols_in,
    speed_cols_in,
    p_cols_in,
    vz_cols_in,
    local_sem,
    send_sem,
    recv_sem,
):
    tiles, subs, rw, rs, nz, cap = dims
    nh = nz // LANES
    shift = nz.bit_length() - 1
    slots = 3 * cap
    a = lax.axis_index("tile")
    c = lax.axis_index("sub")
    has = (a > 0, a < tiles - 1, c > 0, c < subs - 1)
    target = ((a - 1, c), (a + 1, c), (a, c - 1), (a, c + 1))

    barrier = pltpu.get_barrier_semaphore()
    for d in range(4):

        @pl.when(has[d])
        def _():
            pl.semaphore_signal(barrier, inc=1, device_id=target[d], device_id_type=MESH)

    loads = [
        pltpu.make_async_copy(src, dst, local_sem.at[i])
        for i, (src, dst) in enumerate(
            ((water_in, W), (steel_in, S), (water_coef_in, WC), (steel_coef_in, SC))
        )
    ]
    for load in loads:
        load.start()

    ids = {}

    def copy(name, d, src, dst):
        key = (name, d)
        if key not in ids:
            ids[key] = len(ids)
        return pltpu.make_async_remote_copy(
            src_ref=src,
            dst_ref=dst,
            send_sem=send_sem.at[ids[key]],
            recv_sem=recv_sem.at[ids[key]],
            device_id=target[d],
            device_id_type=MESH,
        )

    pending = {}

    def send(name, d, src, dst):
        @pl.when(has[d])
        def _():
            copy(name, d, src, dst).start()

        pending[(name, d)] = (src, dst)

    def arrived(name, d, dst):
        @pl.when(has[d ^ 1])
        def _():
            copy(name, d, dst, dst).wait_recv()

    def sent(name, d):
        src, dst = pending.pop((name, d))

        @pl.when(has[d])
        def _():
            copy(name, d, src, dst).wait_send()

    for d, refs in (
        (0, (lists_in, stress_rows_in, speed_rows_in, p_rows_in, vx_rows_in)),
        (1, (lists_in, stress_rows_in, speed_rows_in, p_rows_in, vx_rows_in)),
        (2, (stress_cols_in, speed_cols_in, p_cols_in, vz_cols_in)),
        (3, (stress_cols_in, speed_cols_in, p_cols_in, vz_cols_in)),
    ):

        @pl.when(jnp.logical_not(has[d ^ 1]))
        def _():
            for ref in refs:
                part = ref.at[d % 2]
                part[...] = jnp.zeros(part.shape, F32)

    lane_row = lambda ref: jnp.concatenate([ref[0:1, :], ref[1:2, :], ref[2:3, :]], axis=1)
    wcell = lane_row(water_cell)
    scell = lane_row(steel_cell)
    code = lane_row(stencil_code)
    slot = lax.broadcasted_iota(jnp.int32, (1, cap), 1)
    live = jnp.concatenate([slot < counts[m, 0] for m in range(3)], axis=1)
    weight = jnp.zeros((1, slots), F32)
    for k in range(9):
        weight = jnp.where(code == k, coupling[k], weight)
    FAC[...] = jnp.where(live, weight, 0.0)

    def selectors(cell, rows, R, L):
        row = cell >> shift
        key = ((cell >> 7) & (nh - 1)) * rows + row
        low = cell & (LANES - 1)
        count = nh * rows
        block = min(128, count)
        for k0 in range(0, count, block):
            index = lax.broadcasted_iota(jnp.int32, (block, slots), 0) + k0
            R[k0 : k0 + block, :] = jnp.where(index == key, 1.0, 0.0).astype(BF16)
        index = lax.broadcasted_iota(jnp.int32, (LANES, slots), 0)
        L[...] = jnp.where(index == low, 1.0, 0.0)

    selectors(wcell, rw, RW, LW)

    def gather(field, rows, R, L):
        stacked = jnp.concatenate(
            [field[:, h * LANES : (h + 1) * LANES] for h in range(nh)], axis=0
        )
        parts = split_two(jnp.transpose(stacked))
        picked = jnp.dot(
            jnp.concatenate(parts, axis=0), R[...], preferred_element_type=F32
        )
        picked = (picked[:LANES] + picked[LANES:]) * L[...]
        return jnp.sum(picked, axis=0, keepdims=True)

    def scatter(values, R, L):
        parts = split_two(L[...] * values)
        spread = lax.dot_general(
            R[...],
            jnp.concatenate(parts, axis=0),
            (((1,), (1,)), ((), ())),
            preferred_element_type=F32,
        )
        return spread[:, :LANES] + spread[:, LANES:]

    def masks(rows):
        row = lax.broadcasted_iota(jnp.int32, (rows, LANES), 0)
        return row == 0, row == rows - 1

    steel_top, steel_bottom = masks(rs)
    water_top, water_bottom = masks(rw)
    at = lambda h: slice(h * LANES, (h + 1) * LANES)

    def send_lists(name, n, values):
        lists_out[0, n] = values[:, :cap]
        lists_out[1, n] = values[:, 2 * cap :]
        for d in (0, 1):
            send(name, d, lists_out.at[d, n], lists_in.at[d, n])

    def receive_lists(name, n, values):
        for d in (0, 1):
            arrived(name, d, lists_in.at[d, n])
        return jnp.concatenate(
            [lists_in[1, n], values[:, cap : 2 * cap], lists_in[0, n]], axis=1
        )

    def send_rows(name, n, fields, rows, out, into):
        for d, r in ((0, 0), (1, rows - 1)):
            for i, (ref, f) in enumerate(fields):
                out[d, n, i] = ref[f, r : r + 1, :]
            send(name, d, out.at[d, n], into.at[d, n])

    def send_cols(name, n, src, into):
        send(name, 2, src[0], into.at[0, n])
        send(name, 3, src[1], into.at[1, n])

    def wait_rows(name, n, into):
        for d in (0, 1):
            arrived(name, d, into.at[d, n])

    def wait_cols(name, n, into):
        for d in (2, 3):
            arrived(name, d, into.at[d - 2, n])

    def all_sent(name, directions):
        for d in directions:
            sent(name, d)

    first, last = slice(0, LANES), slice(nz - LANES, nz)

    def send_stress(n):
        send_rows(f"sr{n}", n, ((S, 2), (S, 4)), rs, stress_rows_out, stress_rows_in)
        send_cols(f"sc{n}", n, (S.at[3:5, :, first], S.at[3:5, :, last]), stress_cols_in)

    def send_speed(n):
        send_rows(f"ur{n}", n, ((S, 0), (S, 1)), rs, speed_rows_out, speed_rows_in)
        send_cols(f"uc{n}", n, (S.at[0:2, :, first], S.at[0:2, :, last]), speed_cols_in)

    def send_p(n):
        send_rows(f"pr{n}", n, ((W, 0),), rw, p_rows_out, p_rows_in)
        send_cols(f"pc{n}", n, (W.at[0, :, first], W.at[0, :, last]), p_cols_in)

    def send_v(n):
        send_rows(f"vr{n}", n, ((W, 1),), rw, vx_rows_out, vx_rows_in)
        send_cols(f"vc{n}", n, (W.at[2, :, first], W.at[2, :, last]), vz_cols_in)

    def columns(ref, f, into, n, i, rows):
        return Columns(
            lambda h: ref[f, :, at(h)],
            (lambda: into[1, n]) if i is None else (lambda: into[1, n, i]),
            (lambda: into[0, n]) if i is None else (lambda: into[0, n, i]),
            nh,
            (rows, LANES),
        )

    def rows_of(ref, f, into, n, i, top, bottom):
        return lambda h: row_difference(
            ref[f, :, at(h)], into[1, n, i, :, at(h)], into[0, n, i, :, at(h)], top, bottom
        )

    def steel_speed(n):
        wait_rows(f"sr{n}", n, stress_rows_in)
        wait_cols(f"sc{n}", n, stress_cols_in)
        dr_xx = rows_of(S, 2, stress_rows_in, n, 0, steel_top, steel_bottom)
        dr_xz = rows_of(S, 4, stress_rows_in, n, 1, steel_top, steel_bottom)
        dc_zz = columns(S, 3, stress_cols_in, n, 0, rs)
        dc_xz = columns(S, 4, stress_cols_in, n, 1, rs)
        for h in range(nh):
            half = 0.5 * SC[0, :, at(h)]
            S[0, :, at(h)] = S[0, :, at(h)] + half * (dr_xx(h) + dc_xz(h))
            S[1, :, at(h)] = S[1, :, at(h)] + half * (dr_xz(h) + dc_zz(h))

    def steel_load(values):
        LOAD[...] = scatter(values, RS, LS)
        for h in range(nh):
            S[1, :, at(h)] = S[1, :, at(h)] - SC[0, :, at(h)] * LOAD[h * rs : (h + 1) * rs, :]

    def steel_stress(n):
        wait_rows(f"ur{n}", n, speed_rows_in)
        wait_cols(f"uc{n}", n, speed_cols_in)
        dr_x = rows_of(S, 0, speed_rows_in, n, 0, steel_top, steel_bottom)
        dr_z = rows_of(S, 1, speed_rows_in, n, 1, steel_top, steel_bottom)
        dc_x = columns(S, 0, speed_cols_in, n, 0, rs)
        dc_z = columns(S, 1, speed_cols_in, n, 1, rs)
        for h in range(nh):
            across, along = 0.5 * dr_x(h), 0.5 * dc_z(h)
            S[2, :, at(h)] = S[2, :, at(h)] + SC[1, :, at(h)] * across + SC[2, :, at(h)] * along
            S[3, :, at(h)] = S[3, :, at(h)] + SC[2, :, at(h)] * across + SC[3, :, at(h)] * along
            S[4, :, at(h)] = S[4, :, at(h)] + (0.5 * SC[4, :, at(h)]) * (dc_x(h) + dr_z(h))

    def water_speed(n):
        wait_rows(f"pr{n}", n, p_rows_in)
        wait_cols(f"pc{n}", n, p_cols_in)
        dr_p = rows_of(W, 0, p_rows_in, n, 0, water_top, water_bottom)
        dc_p = columns(W, 0, p_cols_in, n, None, rw)
        for h in range(nh):
            half = 0.5 * WC[0, :, at(h)]
            W[1, :, at(h)] = W[1, :, at(h)] - half * dr_p(h)
            W[2, :, at(h)] = W[2, :, at(h)] - half * dc_p(h)

    def water_pressure(n):
        wait_rows(f"vr{n}", n, vx_rows_in)
        wait_cols(f"vc{n}", n, vz_cols_in)
        dr_v = rows_of(W, 1, vx_rows_in, n, 0, water_top, water_bottom)
        dc_v = columns(W, 2, vz_cols_in, n, None, rw)
        for h in range(nh):
            W[0, :, at(h)] = W[0, :, at(h)] - (0.5 * WC[1, :, at(h)]) * (dr_v(h) + dc_v(h))

    def water_feed(values):
        fed = scatter(values * FAC[...], RW, LW)
        for h in range(nh):
            W[0, :, at(h)] = W[0, :, at(h)] + fed[h * rw : (h + 1) * rw, :]

    loads[0].wait()
    sample = gather(W.at[0], rw, RW, LW) * FAC[...]
    loads[1].wait()
    pl.semaphore_wait(barrier, sum(h.astype(jnp.int32) for h in has))

    send_stress(0)
    send_lists("s0", 0, sample)
    send_p(0)
    selectors(scell, rs, RS, LS)
    loads[2].wait()
    loads[3].wait()
    for n in range(STEPS):
        steel_speed(n)
        send_speed(n)
        water_speed(n)
        send_v(n)
        all_sent(f"sr{n}", (0, 1))
        all_sent(f"sc{n}", (2, 3))
        all_sent(f"pr{n}", (0, 1))
        all_sent(f"pc{n}", (2, 3))
        steel_load_values = receive_lists(f"s{n}", 2 * n, sample)
        all_sent(f"uc{n}", (2, 3))
        steel_load(steel_load_values)
        steel_stress(n)
        traction = gather(S.at[3], rs, RS, LS)
        send_lists(f"t{n}", 2 * n + 1, traction)
        if n < STEPS - 1:
            send_stress(n + 1)
        water_pressure(n)
        returning = receive_lists(f"t{n}", 2 * n + 1, traction)
        water_feed(returning)
        if n < STEPS - 1:
            sample = gather(W.at[0], rw, RW, LW) * FAC[...]
            send_lists(f"s{n + 1}", 2 * n + 2, sample)
            send_p(n + 1)
        all_sent(f"s{n}", (0, 1))
        all_sent(f"t{n}", (0, 1))
        all_sent(f"ur{n}", (0, 1))
        all_sent(f"vr{n}", (0, 1))
        all_sent(f"vc{n}", (2, 3))
    stores = [
        pltpu.make_async_copy(W, water_out, local_sem.at[0]),
        pltpu.make_async_copy(S, steel_out, local_sem.at[1]),
    ]
    for store in stores:
        store.start()
    for store in stores:
        store.wait()


def on_device(
    tiles,
    subs,
    water_state,
    water_coef,
    steel_state,
    steel_coef,
    coupling,
    water_cell,
    stencil_code,
    link_count,
    steel_cell,
):
    rw, nz = water_state.shape[1:]
    rs = steel_state.shape[1]
    cap = water_cell.shape[1]
    slots = 3 * cap
    nh = nz // LANES
    vmem = pl.BlockSpec(memory_space=pltpu.VMEM)
    smem = pl.BlockSpec(memory_space=pltpu.SMEM)
    anywhere = pl.BlockSpec(memory_space=pl.ANY)
    rows_of = lambda fields: pltpu.VMEM((2, STEPS, fields, 1, nz), F32)
    return pl.pallas_call(
        functools.partial(kernel, (tiles, subs, rw, rs, nz, cap)),
        out_shape=(
            jax.ShapeDtypeStruct(water_state.shape, F32),
            jax.ShapeDtypeStruct(steel_state.shape, F32),
        ),
        in_specs=[smem, smem, vmem, vmem, vmem] + [anywhere] * 4,
        out_specs=(anywhere, anywhere),
        scratch_shapes=[
            pltpu.VMEM(water_state.shape, F32),
            pltpu.VMEM(water_coef.shape, F32),
            pltpu.VMEM(steel_state.shape, F32),
            pltpu.VMEM(steel_coef.shape, F32),
            pltpu.VMEM((nh * rw, slots), BF16),
            pltpu.VMEM((nh * rs, slots), BF16),
            pltpu.VMEM((LANES, slots), F32),
            pltpu.VMEM((LANES, slots), F32),
            pltpu.VMEM((1, slots), F32),
            pltpu.VMEM((nh * rs, LANES), F32),
            pltpu.VMEM((2, 2 * STEPS, 1, cap), F32),
            pltpu.VMEM((2, 2 * STEPS, 1, cap), F32),
            rows_of(2),
            rows_of(2),
            rows_of(2),
            rows_of(2),
            rows_of(1),
            rows_of(1),
            rows_of(1),
            rows_of(1),
            pltpu.VMEM((2, STEPS, 2, rs, LANES), F32),
            pltpu.VMEM((2, STEPS, 2, rs, LANES), F32),
            pltpu.VMEM((2, STEPS, rw, LANES), F32),
            pltpu.VMEM((2, STEPS, rw, LANES), F32),
            pltpu.SemaphoreType.DMA((4,)),
            pltpu.SemaphoreType.DMA((64,)),
            pltpu.SemaphoreType.DMA((64,)),
        ],
        compiler_params=pltpu.CompilerParams(
            collective_id=0, has_side_effects=True, vmem_limit_bytes=48 * 1024 * 1024
        ),
    )(
        coupling,
        link_count,
        water_cell,
        stencil_code,
        steel_cell,
        water_state,
        water_coef,
        steel_state,
        steel_coef,
    )


def solution(mesh):
    in_specs = (
        P(None, "tile", "sub"),
        P(None, "tile", "sub"),
        P(None, "tile", "sub"),
        P(None, "tile", "sub"),
        P(),
        P("tile", "sub"),
        P("tile", "sub"),
        P("tile", "sub"),
        P("tile", "sub"),
    )
    out_specs = (P(None, "tile", "sub"), P(None, "tile", "sub"))
    return jax.shard_map(
        functools.partial(on_device, mesh.shape["tile"], mesh.shape["sub"]),
        mesh=mesh,
        in_specs=in_specs,
        out_specs=out_specs,
        check_vma=False,
    )
```

time: 325 us -> 54.9 us (0.17)
  starting transfers between devices: 196 us -> 0 us
  other arithmetic: 56.7 us -> 0 us
  local copies, waits for them, and re-layouts: 65.4 us -> 9.84 us
  Pallas kernels: 0 us -> 44.1 us
    ppermute x48 -> x0, starting transfers between devices: 196 us -> none  [the longest x24 116 us: padded(): after = lax.ppermute(initial, axis, down)]
    pallas_call x0 -> x1, Pallas kernels: none -> 44.1 us  [on_device(): pl.pallas_call(functools.partial(kernel, (tiles, subs, rw, rs, nz, cap)),...]
    scatter-add x6 -> x0, other arithmetic: 28.5 us -> none  [the longest x3 14.6 us: on_device(): loading = jnp.zeros((steel_rows * steel_columns,), jnp.float32).at[steel_...]
    gather x6 -> x0, local copies, waits for them, and re-layouts: 26.8 us -> none  [the longest x3 13.4 us: on_device(): water_state[0].reshape(-1)[water_flat].reshape(factor.shape) * factor]
    concatenate x9 -> x0, local copies, waits for them, and re-layouts: 14.7 us -> none  [padded(): array = jnp.concatenate([before, array, after], axis=dim)]
    squeeze x9 -> x0, local copies, waits for them, and re-layouts: 8.95 us -> none  [the longest x3 3.71 us: steel_update(): velocity_z = extended[1]]
    concatenate x12 -> x0, other arithmetic: 7.69 us -> none  [the longest x9 4.28 us: padded(): array = jnp.concatenate([before, array, after], axis=dim)]
    another operation x9 -> x0, other arithmetic: 6.85 us -> none  [the longest x3 5.53 us: steel_update(): jnp.stack([moved_x, moved_z])]
  transfers between devices with their start and end apart: 48 -> 0, of which waited for: 3 -> 0; matrix products, arithmetic and copies ran while one was open for 27% -> 0% of each run, Pallas kernels for 0% -> 0%
where the time goes in v1:
time: 54.9 us; the launch traced here: 54.6 us
  Pallas kernels  44.1 us (80%)
  local copies, waits for them, and re-layouts  9.84 us (18%)
  between operations  0.65 us (1%)
    pallas_call x1, Pallas kernels, on_device(): pl.pallas_call(functools.partial(kernel, (tiles, subs, rw, rs, nz, cap)),...  44.1 us
    unnamed x19, local copies, waits for them, and re-layouts  9.84 us

profile of v1, /device:TPU:25, one launch (start us, length us, event | category | flops | bytes accessed | tf_op | source)
XLA Modules:
  0.0 54.6 jit_solution(15902215319339227537)
XLA Ops:
  0.6 0.7 %copy.11.counts = s32[3,1]{1,0:T(4,128)S(1)} copy(s32[3,1]{0,1:T(1,128)} %param.16) | data formatting | bytes 24 | tf_op args[7]
  1.4 0.0 copy-start
  1.4 1.3 %copy-done = f32[5,16,4096]{2,1,0:T(8,128)S(1)} copy-done((f32[5,16,4096]{2,1,0:T(8,128)S(1)}, f32[5,16,4096]{2,1,0:T(8,128)}, u32[]{:S(2)}) %copy-start) | copy-done | bytes 1310744
  2.7 0.0 copy-start.1
  2.7 1.3 %copy-done.1 = f32[5,16,4096]{2,1,0:T(8,128)S(1)} copy-done((f32[5,16,4096]{2,1,0:T(8,128)S(1)}, f32[5,16,4096]{2,1,0:T(8,128)}, u32[]{:S(2)}) %copy-start.1) | copy-done | bytes 1310744
  4.0 0.0 copy-start.2
  4.0 1.0 %copy-done.2 = f32[3,8,4096]{2,1,0:T(8,128)S(1)} copy-done((f32[3,8,4096]{2,1,0:T(8,128)S(1)}, f32[3,8,4096]{2,1,0:T(8,128)}, u32[]{:S(2)}) %copy-start.2) | copy-done | bytes 393240
  5.0 0.0 copy-start.3
  5.0 0.9 %copy-done.3 = f32[2,8,4096]{2,1,0:T(8,128)S(1)} copy-done((f32[2,8,4096]{2,1,0:T(8,128)S(1)}, f32[2,8,4096]{2,1,0:T(8,128)}, u32[]{:S(2)}) %copy-start.3) | copy-done | bytes 262168
  6.0 0.0 copy-start.4
  6.0 0.7 %copy-done.4 = s32[3,256]{1,0:T(4,128)S(1)} copy-done((s32[3,256]{1,0:T(4,128)S(1)}, s32[3,256]{1,0:T(4,128)}, u32[]{:S(2)}) %copy-start.4) | copy-done | bytes 3096
  6.6 0.0 copy-start.5
  6.6 0.7 %copy-done.5 = s32[3,256]{1,0:T(4,128)S(1)} copy-done((s32[3,256]{1,0:T(4,128)S(1)}, s32[3,256]{1,0:T(4,128)}, u32[]{:S(2)}) %copy-start.5) | copy-done | bytes 3096
  7.3 0.0 copy-start.6
  7.3 0.7 %copy-done.6 = s32[3,256]{1,0:T(4,128)S(1)} copy-done((s32[3,256]{1,0:T(4,128)S(1)}, s32[3,256]{1,0:T(4,128)}, u32[]{:S(2)}) %copy-start.6) | copy-done | bytes 3096
  8.0 0.0 copy-start.7
  8.0 0.7 %copy-done.7 = f32[9]{0:T(128)S(1)} copy-done((f32[9]{0:T(128)S(1)}, f32[9]{0:T(128)}, u32[]{:S(2)}) %copy-start.7) | copy-done | bytes 60
  8.7 44.1 %shard_map.104 = (f32[3,8,4096]{2,1,0:T(8,128)S(1)}, f32[5,16,4096]{2,1,0:T(8,128)S(1)}) custom-call(f32[9]{0:T(128)S(1)} %copy-done.7, s32[3,1]{1,0:T(4,128)S(1)} %copy.11.counts, s32[3,256]{1,0:T(4,128)S(1)} %copy-done.4, s32[3,256]{1,0:T(4,128)S(1)} %copy-done.5, s32[3,256]{1,0:T(4,128)S(1)} %copy-done.6, f32[3,8,4096]{2,1,0:T(8,128)S(1)} %copy-done.2, ...), custom_call_target="tpu_custom_call" | custom-call | tf_op jit(solution)/shard_map/pallas_call | solution.py:417
  52.8 0.7 %copy.14 = f32[3,8,4096]{2,1,0:T(8,128)} copy(f32[3,8,4096]{2,1,0:T(8,128)S(1)} %get-tuple-element.4) | data formatting | bytes 786432
  53.5 1.1 %copy.15 = f32[5,16,4096]{2,1,0:T(8,128)} copy(f32[5,16,4096]{2,1,0:T(8,128)S(1)} %get-tuple-element.5) | data formatting | bytes 2621440
Async XLA Ops:
  1.4 1.3 %copy-start = (f32[5,16,4096]{2,1,0:T(8,128)S(1)}, f32[5,16,4096]{2,1,0:T(8,128)}, u32[]{:S(2)}) copy-start(f32[5,16,4096]{2,1,0:T(8,128)} %steel_in.1) | copy-start | bytes 3932164
  2.7 1.3 %copy-start.1 = (f32[5,16,4096]{2,1,0:T(8,128)S(1)}, f32[5,16,4096]{2,1,0:T(8,128)}, u32[]{:S(2)}) copy-start(f32[5,16,4096]{2,1,0:T(8,128)} %steel_coef_in.1) | copy-start | bytes 3932164
  4.0 1.0 %copy-start.2 = (f32[3,8,4096]{2,1,0:T(8,128)S(1)}, f32[3,8,4096]{2,1,0:T(8,128)}, u32[]{:S(2)}) copy-start(f32[3,8,4096]{2,1,0:T(8,128)} %water_in.1) | copy-start | bytes 1179652
  5.0 0.9 %copy-start.3 = (f32[2,8,4096]{2,1,0:T(8,128)S(1)}, f32[2,8,4096]{2,1,0:T(8,128)}, u32[]{:S(2)}) copy-start(f32[2,8,4096]{2,1,0:T(8,128)} %water_coef_in.1) | copy-start | bytes 786436
  6.0 0.7 %copy-start.4 = (s32[3,256]{1,0:T(4,128)S(1)}, s32[3,256]{1,0:T(4,128)}, u32[]{:S(2)}) copy-start(s32[3,256]{1,0:T(4,128)} %water_cell.1) | copy-start | bytes 9220
  6.6 0.7 %copy-start.5 = (s32[3,256]{1,0:T(4,128)S(1)}, s32[3,256]{1,0:T(4,128)}, u32[]{:S(2)}) copy-start(s32[3,256]{1,0:T(4,128)} %stencil_code.1) | copy-start | bytes 9220
  7.3 0.7 %copy-start.6 = (s32[3,256]{1,0:T(4,128)S(1)}, s32[3,256]{1,0:T(4,128)}, u32[]{:S(2)}) copy-start(s32[3,256]{1,0:T(4,128)} %steel_cell.1) | copy-start | bytes 9220
  8.0 0.7 %copy-start.7 = (f32[9]{0:T(128)S(1)}, f32[9]{0:T(128)}, u32[]{:S(2)}) copy-start(f32[9]{0:T(128)} %coupling.1) | copy-start | bytes 112

commit v2 on v1

--- a/solution.py
+++ b/solution.py
@@ -10,6 +10,7 @@
 MESH = pl.DeviceIdType.MESH
 STEPS = 3
 LANES = 128
+VMEM_BYTES = 67043328
 F32 = jnp.float32
 BF16 = jnp.bfloat16
 
@@ -55,20 +56,23 @@
 
 def kernel(
     dims,
+    coupling_in,
+    counts_in,
+    water_cell_in,
+    stencil_code_in,
+    steel_cell_in,
+    water_in,
+    water_coef_in,
+    steel_in,
+    steel_coef_in,
+    W,
+    S,
     coupling,
     counts,
     water_cell,
     stencil_code,
     steel_cell,
-    water_in,
-    water_coef_in,
-    steel_in,
-    steel_coef_in,
-    water_out,
-    steel_out,
-    W,
     WC,
-    S,
     SC,
     RW,
     RS,
@@ -113,7 +117,17 @@
     loads = [
         pltpu.make_async_copy(src, dst, local_sem.at[i])
         for i, (src, dst) in enumerate(
-            ((water_in, W), (steel_in, S), (water_coef_in, WC), (steel_coef_in, SC))
+            (
+                (coupling_in, coupling),
+                (counts_in, counts),
+                (stencil_code_in, stencil_code),
+                (water_cell_in, water_cell),
+                (water_in, W),
+                (steel_cell_in, steel_cell),
+                (steel_in, S),
+                (water_coef_in, WC),
+                (steel_coef_in, SC),
+            )
         )
     ]
     for load in loads:
@@ -168,12 +182,13 @@
                 part = ref.at[d % 2]
                 part[...] = jnp.zeros(part.shape, F32)
 
+    for load in loads[:4]:
+        load.wait()
     lane_row = lambda ref: jnp.concatenate([ref[0:1, :], ref[1:2, :], ref[2:3, :]], axis=1)
     wcell = lane_row(water_cell)
-    scell = lane_row(steel_cell)
     code = lane_row(stencil_code)
     slot = lax.broadcasted_iota(jnp.int32, (1, cap), 1)
-    live = jnp.concatenate([slot < counts[m, 0] for m in range(3)], axis=1)
+    live = jnp.concatenate([slot < counts[0, m] for m in range(3)], axis=1)
     weight = jnp.zeros((1, slots), F32)
     for k in range(9):
         weight = jnp.where(code == k, coupling[k], weight)
@@ -342,17 +357,18 @@
         for h in range(nh):
             W[0, :, at(h)] = W[0, :, at(h)] + fed[h * rw : (h + 1) * rw, :]
 
-    loads[0].wait()
+    loads[4].wait()
     sample = gather(W.at[0], rw, RW, LW) * FAC[...]
-    loads[1].wait()
+    loads[6].wait()
     pl.semaphore_wait(barrier, sum(h.astype(jnp.int32) for h in has))
 
     send_stress(0)
     send_lists("s0", 0, sample)
     send_p(0)
-    selectors(scell, rs, RS, LS)
-    loads[2].wait()
-    loads[3].wait()
+    loads[5].wait()
+    selectors(lane_row(steel_cell), rs, RS, LS)
+    loads[7].wait()
+    loads[8].wait()
     for n in range(STEPS):
         steel_speed(n)
         send_speed(n)
@@ -382,9 +398,12 @@
         all_sent(f"ur{n}", (0, 1))
         all_sent(f"vr{n}", (0, 1))
         all_sent(f"vc{n}", (2, 3))
+
+
+def store_kernel(water, steel, water_out, steel_out, sem):
     stores = [
-        pltpu.make_async_copy(W, water_out, local_sem.at[0]),
-        pltpu.make_async_copy(S, steel_out, local_sem.at[1]),
+        pltpu.make_async_copy(steel, steel_out, sem.at[0]),
+        pltpu.make_async_copy(water, water_out, sem.at[1]),
     ]
     for store in stores:
         store.start()
@@ -411,21 +430,23 @@
     slots = 3 * cap
     nh = nz // LANES
     vmem = pl.BlockSpec(memory_space=pltpu.VMEM)
-    smem = pl.BlockSpec(memory_space=pltpu.SMEM)
-    anywhere = pl.BlockSpec(memory_space=pl.ANY)
+    hbm = pl.BlockSpec(memory_space=pltpu.HBM)
     rows_of = lambda fields: pltpu.VMEM((2, STEPS, fields, 1, nz), F32)
-    return pl.pallas_call(
+    results = pl.pallas_call(
         functools.partial(kernel, (tiles, subs, rw, rs, nz, cap)),
         out_shape=(
-            jax.ShapeDtypeStruct(water_state.shape, F32),
-            jax.ShapeDtypeStruct(steel_state.shape, F32),
+            pltpu.VMEM(water_state.shape, F32),
+            pltpu.VMEM(steel_state.shape, F32),
         ),
-        in_specs=[smem, smem, vmem, vmem, vmem] + [anywhere] * 4,
-        out_specs=(anywhere, anywhere),
+        in_specs=[hbm] * 9,
+        out_specs=(vmem, vmem),
         scratch_shapes=[
-            pltpu.VMEM(water_state.shape, F32),
+            pltpu.SMEM(coupling.shape, F32),
+            pltpu.SMEM((1, 3), jnp.int32),
+            pltpu.VMEM(water_cell.shape, jnp.int32),
+            pltpu.VMEM(water_cell.shape, jnp.int32),
+            pltpu.VMEM(water_cell.shape, jnp.int32),
             pltpu.VMEM(water_coef.shape, F32),
-            pltpu.VMEM(steel_state.shape, F32),
             pltpu.VMEM(steel_coef.shape, F32),
             pltpu.VMEM((nh * rw, slots), BF16),
             pltpu.VMEM((nh * rs, slots), BF16),
@@ -447,16 +468,16 @@
             pltpu.VMEM((2, STEPS, 2, rs, LANES), F32),
             pltpu.VMEM((2, STEPS, rw, LANES), F32),
             pltpu.VMEM((2, STEPS, rw, LANES), F32),
-            pltpu.SemaphoreType.DMA((4,)),
+            pltpu.SemaphoreType.DMA((9,)),
             pltpu.SemaphoreType.DMA((64,)),
             pltpu.SemaphoreType.DMA((64,)),
         ],
         compiler_params=pltpu.CompilerParams(
-            collective_id=0, has_side_effects=True, vmem_limit_bytes=48 * 1024 * 1024
+            collective_id=0, has_side_effects=True, vmem_limit_bytes=VMEM_BYTES - 4 * (water_state.size + steel_state.size)
         ),
     )(
         coupling,
-        link_count,
+        link_count.reshape(1, 3),
         water_cell,
         stencil_code,
         steel_cell,
@@ -465,6 +486,17 @@
         steel_state,
         steel_coef,
     )
+    return pl.pallas_call(
+        store_kernel,
+        out_shape=(
+            jax.ShapeDtypeStruct(water_state.shape, F32),
+            jax.ShapeDtypeStruct(steel_state.shape, F32),
+        ),
+        in_specs=[vmem, vmem],
+        out_specs=(hbm, hbm),
+        scratch_shapes=[pltpu.SemaphoreType.DMA((2,))],
+        compiler_params=pltpu.CompilerParams(vmem_limit_bytes=1024 * 1024),
+    )(*results)
 
 
 def solution(mesh):

time: 54.9 us -> 45.8 us (0.83)
  local copies, waits for them, and re-layouts: 9.84 us -> 0 us
    unnamed x19 -> x0, local copies, waits for them, and re-layouts: 9.84 us -> none
    pallas_call x0 -> x1, Pallas kernels: none -> 1.2 us  [on_device(): pl.pallas_call(store_kernel, out_shape=(jax.ShapeDtypeStruct(water_state....]
    pallas_call x1, Pallas kernels: 44.1 us -> 43.3 us  [on_device(): pl.pallas_call(functools.partial(kernel, (tiles, subs, rw, rs, nz, cap)),...]
where the time goes in v2:
time: 45.8 us; the launch traced here: 45.1 us
  Pallas kernels  44.5 us (97%)
  between operations  0.64 us (1%)
    pallas_call x1, Pallas kernels, on_device(): pl.pallas_call(functools.partial(kernel, (tiles, subs, rw, rs, nz, cap)),...  43.3 us
    pallas_call x1, Pallas kernels, on_device(): pl.pallas_call(store_kernel, out_shape=(jax.ShapeDtypeStruct(water_state....  1.2 us

profile of v2, /device:TPU:25, one launch (start us, length us, event | category | flops | bytes accessed | tf_op | source)
XLA Modules:
  0.0 45.1 jit_solution(18399355745309818970)
XLA Ops:
  0.6 43.3 %shard_map.104 = (f32[3,8,4096]{2,1,0:T(8,128)S(1)}, f32[5,16,4096]{2,1,0:T(8,128)S(1)}) custom-call(f32[9]{0:T(128)} %coupling_in.1, s32[1,3]{1,0:T(1,128)} %bitcast.1, s32[3,256]{1,0:T(4,128)} %water_cell_in.1, s32[3,256]{1,0:T(4,128)} %stencil_code_in.1, s32[3,256]{1,0:T(4,128)} %steel_cell_in.1, f32[3,8,4096]{2,1,0:T(8,128)} %water_in.1, ...), custom_call_target="tpu_custom_call" | custom-call | tf_op jit(solution)/shard_map/pallas_call | solution.py:435
  43.9 1.2 %shard_map.105 = (f32[3,8,4096]{2,1,0:T(8,128)}, f32[5,16,4096]{2,1,0:T(8,128)}) custom-call(f32[3,8,4096]{2,1,0:T(8,128)S(1)} %get-tuple-element.4.water, f32[5,16,4096]{2,1,0:T(8,128)S(1)} %get-tuple-element.5.steel), custom_call_target="tpu_custom_call" | custom-call | tf_op jit(solution)/shard_map/pallas_call | solution.py:489

commit v3 on v2

--- a/solution.py
+++ b/solution.py
@@ -85,15 +85,16 @@
     stress_rows_out,
     stress_rows_in,
     speed_rows_out,
-    speed_rows_in,
+    speed_rows,
     p_rows_out,
     p_rows_in,
     vx_rows_out,
-    vx_rows_in,
+    vx_rows,
     stress_cols_in,
-    speed_cols_in,
+    speed_cols,
     p_cols_in,
-    vz_cols_in,
+    vz_cols,
+    corners_in,
     local_sem,
     send_sem,
     recv_sem,
@@ -104,11 +105,17 @@
     slots = 3 * cap
     a = lax.axis_index("tile")
     c = lax.axis_index("sub")
-    has = (a > 0, a < tiles - 1, c > 0, c < subs - 1)
-    target = ((a - 1, c), (a + 1, c), (a, c - 1), (a, c + 1))
+    moves = ((-1, 0), (1, 0), (0, -1), (0, 1), (-1, -1), (-1, 1), (1, -1), (1, 1))
+    opposite = (1, 0, 3, 2, 7, 6, 5, 4)
+    along = {(0, -1): c > 0, (0, 1): c < subs - 1, (-1, 0): a > 0, (1, 0): a < tiles - 1}
+    has = [
+        along[m] if m in along else jnp.logical_and(along[(m[0], 0)], along[(0, m[1])])
+        for m in moves
+    ]
+    target = [(a + m[0], c + m[1]) for m in moves]
 
     barrier = pltpu.get_barrier_semaphore()
-    for d in range(4):
+    for d in range(8):
 
         @pl.when(has[d])
         def _():
@@ -158,7 +165,7 @@
         pending[(name, d)] = (src, dst)
 
     def arrived(name, d, dst):
-        @pl.when(has[d ^ 1])
+        @pl.when(has[opposite[d]])
         def _():
             copy(name, d, dst, dst).wait_recv()
 
@@ -169,17 +176,14 @@
         def _():
             copy(name, d, src, dst).wait_send()
 
-    for d, refs in (
-        (0, (lists_in, stress_rows_in, speed_rows_in, p_rows_in, vx_rows_in)),
-        (1, (lists_in, stress_rows_in, speed_rows_in, p_rows_in, vx_rows_in)),
-        (2, (stress_cols_in, speed_cols_in, p_cols_in, vz_cols_in)),
-        (3, (stress_cols_in, speed_cols_in, p_cols_in, vz_cols_in)),
-    ):
-
-        @pl.when(jnp.logical_not(has[d ^ 1]))
+    row_refs = (lists_in, stress_rows_in, speed_rows, p_rows_in, vx_rows)
+    col_refs = (stress_cols_in, speed_cols, p_cols_in, vz_cols)
+    for d in range(8):
+
+        @pl.when(jnp.logical_not(has[opposite[d]]))
         def _():
-            for ref in refs:
-                part = ref.at[d % 2]
+            for ref in row_refs if d < 2 else col_refs if d < 4 else (corners_in,):
+                part = ref.at[d if d < 2 else d - 2 if d < 4 else d - 4]
                 part[...] = jnp.zeros(part.shape, F32)
 
     for load in loads[:4]:
@@ -250,67 +254,143 @@
             [lists_in[1, n], values[:, cap : 2 * cap], lists_in[0, n]], axis=1
         )
 
-    def send_rows(name, n, fields, rows, out, into):
-        for d, r in ((0, 0), (1, rows - 1)):
-            for i, (ref, f) in enumerate(fields):
-                out[d, n, i] = ref[f, r : r + 1, :]
-            send(name, d, out.at[d, n], into.at[d, n])
-
-    def send_cols(name, n, src, into):
-        send(name, 2, src[0], into.at[0, n])
-        send(name, 3, src[1], into.at[1, n])
-
-    def wait_rows(name, n, into):
-        for d in (0, 1):
-            arrived(name, d, into.at[d, n])
-
-    def wait_cols(name, n, into):
+    first, last = slice(0, LANES), slice(nz - LANES, nz)
+    stress_rows = ((2, 0), (4, 0), (3, 0), (2, 1), (4, 1))
+
+    def put_row(out, ref, f, r):
+        for h in range(nh):
+            out[h : h + 1, :] = ref[f, r : r + 1, at(h)]
+
+    def send_stress(n):
+        for d in (0, 1):
+            for i, (f, r) in enumerate(stress_rows):
+                put_row(stress_rows_out.at[d, n, i], S, f, rs - 1 - r if d else r)
+            send(f"sr{n}", d, stress_rows_out.at[d, n], stress_rows_in.at[d, n])
+        for d, lanes in ((2, first), (3, last)):
+            send(f"sc{n}", d, S.at[2:5, :, lanes], stress_cols_in.at[d - 2, n])
+        for d in range(4, 8):
+            rows = slice(0, 8) if moves[d][0] < 0 else slice(rs - 8, rs)
+            lanes = first if moves[d][1] < 0 else last
+            send(f"sd{n}", d, S.at[2:5, rows, lanes], corners_in.at[d - 4, n])
+
+    def send_speed():
+        for d in (0, 1):
+            for i, (ref, f) in enumerate(((S, 0), (S, 1), (SC, 0))):
+                put_row(speed_rows_out.at[d, i], ref, f, rs - 1 if d else 0)
+            send("ur", d, speed_rows_out.at[d], speed_rows.at[d])
+        for d, lanes in ((2, first), (3, last)):
+            send("uc", d, S.at[0:2, :, lanes], speed_cols.at[d - 2, 0:2])
+            send("bc", d, SC.at[0:1, :, lanes], speed_cols.at[d - 2, 2:3])
+
+    def send_p(n):
+        for d in (0, 1):
+            for r in (0, 1):
+                put_row(p_rows_out.at[d, n, r], W, 0, rw - 1 - r if d else r)
+            send(f"pr{n}", d, p_rows_out.at[d, n], p_rows_in.at[d, n])
+        for d, lanes in ((2, first), (3, last)):
+            send(f"pc{n}", d, W.at[0, :, lanes], p_cols_in.at[d - 2, n])
+
+    def send_v():
+        for d in (0, 1):
+            for i, (ref, f) in enumerate(((W, 1), (WC, 0))):
+                put_row(vx_rows_out.at[d, i], ref, f, rw - 1 if d else 0)
+            send("vr", d, vx_rows_out.at[d], vx_rows.at[d])
+        for d, lanes in ((2, first), (3, last)):
+            send("vc", d, W.at[2:3, :, lanes], vz_cols.at[d - 2, 0:1])
+            send("wc", d, WC.at[0:1, :, lanes], vz_cols.at[d - 2, 1:2])
+
+    def wait_stress(n):
+        for d in (0, 1):
+            arrived(f"sr{n}", d, stress_rows_in.at[d, n])
         for d in (2, 3):
-            arrived(name, d, into.at[d - 2, n])
+            arrived(f"sc{n}", d, stress_cols_in.at[d - 2, n])
+        for d in range(4, 8):
+            arrived(f"sd{n}", d, corners_in.at[d - 4, n])
+
+    def wait_speed():
+        for d in (0, 1):
+            arrived("ur", d, speed_rows.at[d])
+        for d in (2, 3):
+            arrived("uc", d, speed_cols.at[d - 2, 0:2])
+            arrived("bc", d, speed_cols.at[d - 2, 2:3])
+
+    def wait_p(n):
+        for d in (0, 1):
+            arrived(f"pr{n}", d, p_rows_in.at[d, n])
+        for d in (2, 3):
+            arrived(f"pc{n}", d, p_cols_in.at[d - 2, n])
+
+    def wait_v():
+        for d in (0, 1):
+            arrived("vr", d, vx_rows.at[d])
+        for d in (2, 3):
+            arrived("vc", d, vz_cols.at[d - 2, 0:1])
+            arrived("wc", d, vz_cols.at[d - 2, 1:2])
 
     def all_sent(name, directions):
         for d in directions:
             sent(name, d)
 
-    first, last = slice(0, LANES), slice(nz - LANES, nz)
-
-    def send_stress(n):
-        send_rows(f"sr{n}", n, ((S, 2), (S, 4)), rs, stress_rows_out, stress_rows_in)
-        send_cols(f"sc{n}", n, (S.at[3:5, :, first], S.at[3:5, :, last]), stress_cols_in)
-
-    def send_speed(n):
-        send_rows(f"ur{n}", n, ((S, 0), (S, 1)), rs, speed_rows_out, speed_rows_in)
-        send_cols(f"uc{n}", n, (S.at[0:2, :, first], S.at[0:2, :, last]), speed_cols_in)
-
-    def send_p(n):
-        send_rows(f"pr{n}", n, ((W, 0),), rw, p_rows_out, p_rows_in)
-        send_cols(f"pc{n}", n, (W.at[0, :, first], W.at[0, :, last]), p_cols_in)
-
-    def send_v(n):
-        send_rows(f"vr{n}", n, ((W, 1),), rw, vx_rows_out, vx_rows_in)
-        send_cols(f"vc{n}", n, (W.at[2, :, first], W.at[2, :, last]), vz_cols_in)
-
-    def columns(ref, f, into, n, i, rows):
+    def columns(ref, f, into, rows):
         return Columns(
-            lambda h: ref[f, :, at(h)],
-            (lambda: into[1, n]) if i is None else (lambda: into[1, n, i]),
-            (lambda: into[0, n]) if i is None else (lambda: into[0, n, i]),
-            nh,
-            (rows, LANES),
-        )
-
-    def rows_of(ref, f, into, n, i, top, bottom):
+            lambda h: ref[f, :, at(h)], lambda: into(1), lambda: into(0), nh, (rows, LANES)
+        )
+
+    def rows_of(ref, f, into, top, bottom):
         return lambda h: row_difference(
-            ref[f, :, at(h)], into[1, n, i, :, at(h)], into[0, n, i, :, at(h)], top, bottom
-        )
+            ref[f, :, at(h)], into(1)[h : h + 1, :], into(0)[h : h + 1, :], top, bottom
+        )
+
+    line = lax.broadcasted_iota(jnp.int32, (nh, LANES), 0)
+    lane = lax.broadcasted_iota(jnp.int32, (nh, LANES), 1)
+
+    def along_row(x, left, right):
+        before, after = pltpu.roll(x, 1, 1), pltpu.roll(x, LANES - 1, 1)
+        wrapped = jnp.where(line == 0, pltpu.roll(left, 1, 1), pltpu.roll(before, 1, 0))
+        previous = jnp.where(lane == 0, wrapped, before)
+        wrapped = jnp.where(
+            line == nh - 1, pltpu.roll(right, LANES - 1, 1), pltpu.roll(after, nh - 1, 0)
+        )
+        return jnp.where(lane == LANES - 1, wrapped, after) - previous
+
+    def beside(side, tile, ref, f):
+        if side:
+            return pltpu.roll(ref[f, :, first], LANES - 1, 1) - pltpu.roll(tile, 1, 1)
+        return pltpu.roll(tile, LANES - 1, 1) - pltpu.roll(ref[f, :, last], 1, 1)
+
+    def corner(up, left, n, i):
+        r = 7 if up else 0
+        return corners_in[2 * up + left, n, i, r : r + 1, :]
+
+    def outer_speed(n):
+        for side in (1, 0):
+            near = stress_rows_out[1 - side, n]
+            far = stress_rows_in[side, n]
+            half = 0.5 * speed_rows[side, 2]
+            for i, (own, beyond, flat, field) in enumerate(((0, 3, 1, 2), (1, 4, 2, 1))):
+                across = near[own] - far[beyond] if side else far[beyond] - near[own]
+                change = along_row(far[flat], corner(side, 1, n, field), corner(side, 0, n, field))
+                speed_rows[side, i] = speed_rows[side, i] + half * (across + change)
+        for side in (1, 0):
+            half = 0.5 * speed_cols[side, 2]
+            for i, (down, flat) in enumerate(((0, 2), (2, 1))):
+                across = row_difference(
+                    stress_cols_in[side, n, down],
+                    corner(1, side, n, down),
+                    corner(0, side, n, down),
+                    steel_top,
+                    steel_bottom,
+                )
+                change = beside(side, stress_cols_in[side, n, flat], S, flat + 2)
+                speed_cols[side, i] = speed_cols[side, i] + half * (across + change)
 
     def steel_speed(n):
-        wait_rows(f"sr{n}", n, stress_rows_in)
-        wait_cols(f"sc{n}", n, stress_cols_in)
-        dr_xx = rows_of(S, 2, stress_rows_in, n, 0, steel_top, steel_bottom)
-        dr_xz = rows_of(S, 4, stress_rows_in, n, 1, steel_top, steel_bottom)
-        dc_zz = columns(S, 3, stress_cols_in, n, 0, rs)
-        dc_xz = columns(S, 4, stress_cols_in, n, 1, rs)
+        rows_in = lambda i: lambda side: stress_rows_in.at[side, n, i]
+        cols_in = lambda i: lambda side: stress_cols_in[side, n, i]
+        dr_xx = rows_of(S, 2, rows_in(0), steel_top, steel_bottom)
+        dr_xz = rows_of(S, 4, rows_in(1), steel_top, steel_bottom)
+        dc_zz = columns(S, 3, cols_in(1), rs)
+        dc_xz = columns(S, 4, cols_in(2), rs)
         for h in range(nh):
             half = 0.5 * SC[0, :, at(h)]
             S[0, :, at(h)] = S[0, :, at(h)] + half * (dr_xx(h) + dc_xz(h))
@@ -321,13 +401,13 @@
         for h in range(nh):
             S[1, :, at(h)] = S[1, :, at(h)] - SC[0, :, at(h)] * LOAD[h * rs : (h + 1) * rs, :]
 
-    def steel_stress(n):
-        wait_rows(f"ur{n}", n, speed_rows_in)
-        wait_cols(f"uc{n}", n, speed_cols_in)
-        dr_x = rows_of(S, 0, speed_rows_in, n, 0, steel_top, steel_bottom)
-        dr_z = rows_of(S, 1, speed_rows_in, n, 1, steel_top, steel_bottom)
-        dc_x = columns(S, 0, speed_cols_in, n, 0, rs)
-        dc_z = columns(S, 1, speed_cols_in, n, 1, rs)
+    def steel_stress():
+        rows_in = lambda i: lambda side: speed_rows.at[side, i]
+        cols_in = lambda i: lambda side: speed_cols[side, i]
+        dr_x = rows_of(S, 0, rows_in(0), steel_top, steel_bottom)
+        dr_z = rows_of(S, 1, rows_in(1), steel_top, steel_bottom)
+        dc_x = columns(S, 0, cols_in(0), rs)
+        dc_z = columns(S, 1, cols_in(1), rs)
         for h in range(nh):
             across, along = 0.5 * dr_x(h), 0.5 * dc_z(h)
             S[2, :, at(h)] = S[2, :, at(h)] + SC[1, :, at(h)] * across + SC[2, :, at(h)] * along
@@ -335,20 +415,22 @@
             S[4, :, at(h)] = S[4, :, at(h)] + (0.5 * SC[4, :, at(h)]) * (dc_x(h) + dr_z(h))
 
     def water_speed(n):
-        wait_rows(f"pr{n}", n, p_rows_in)
-        wait_cols(f"pc{n}", n, p_cols_in)
-        dr_p = rows_of(W, 0, p_rows_in, n, 0, water_top, water_bottom)
-        dc_p = columns(W, 0, p_cols_in, n, None, rw)
+        for side in (1, 0):
+            near, far = p_rows_out[1 - side, n, 0], p_rows_in[side, n, 1]
+            across = near - far if side else far - near
+            vx_rows[side, 0] = vx_rows[side, 0] - (0.5 * vx_rows[side, 1]) * across
+            change = beside(side, p_cols_in[side, n], W, 0)
+            vz_cols[side, 0] = vz_cols[side, 0] - (0.5 * vz_cols[side, 1]) * change
+        dr_p = rows_of(W, 0, lambda side: p_rows_in.at[side, n, 0], water_top, water_bottom)
+        dc_p = columns(W, 0, lambda side: p_cols_in[side, n], rw)
         for h in range(nh):
             half = 0.5 * WC[0, :, at(h)]
             W[1, :, at(h)] = W[1, :, at(h)] - half * dr_p(h)
             W[2, :, at(h)] = W[2, :, at(h)] - half * dc_p(h)
 
-    def water_pressure(n):
-        wait_rows(f"vr{n}", n, vx_rows_in)
-        wait_cols(f"vc{n}", n, vz_cols_in)
-        dr_v = rows_of(W, 1, vx_rows_in, n, 0, water_top, water_bottom)
-        dc_v = columns(W, 2, vz_cols_in, n, None, rw)
+    def water_pressure():
+        dr_v = rows_of(W, 1, lambda side: vx_rows.at[side, 0], water_top, water_bottom)
+        dc_v = columns(W, 2, lambda side: vz_cols[side, 0], rw)
         for h in range(nh):
             W[0, :, at(h)] = W[0, :, at(h)] - (0.5 * WC[1, :, at(h)]) * (dr_v(h) + dc_v(h))
 
@@ -361,43 +443,46 @@
     sample = gather(W.at[0], rw, RW, LW) * FAC[...]
     loads[6].wait()
     pl.semaphore_wait(barrier, sum(h.astype(jnp.int32) for h in has))
-
+    send_lists("s0", 0, sample)
     send_stress(0)
-    send_lists("s0", 0, sample)
+    loads[8].wait()
+    send_speed()
+    loads[7].wait()
     send_p(0)
+    send_v()
     loads[5].wait()
     selectors(lane_row(steel_cell), rs, RS, LS)
-    loads[7].wait()
-    loads[8].wait()
     for n in range(STEPS):
+        wait_stress(n)
+        if n == 0:
+            wait_speed()
+            all_sent("uc", (2, 3))
+        outer_speed(n)
         steel_speed(n)
-        send_speed(n)
-        water_speed(n)
-        send_v(n)
-        all_sent(f"sr{n}", (0, 1))
+        loading = receive_lists(f"s{n}", 2 * n, sample)
         all_sent(f"sc{n}", (2, 3))
-        all_sent(f"pr{n}", (0, 1))
-        all_sent(f"pc{n}", (2, 3))
-        steel_load_values = receive_lists(f"s{n}", 2 * n, sample)
-        all_sent(f"uc{n}", (2, 3))
-        steel_load(steel_load_values)
-        steel_stress(n)
+        all_sent(f"sd{n}", range(4, 8))
+        steel_load(loading)
+        steel_stress()
         traction = gather(S.at[3], rs, RS, LS)
         send_lists(f"t{n}", 2 * n + 1, traction)
         if n < STEPS - 1:
             send_stress(n + 1)
-        water_pressure(n)
+        wait_p(n)
+        if n == 0:
+            wait_v()
+            all_sent("vc", (2, 3))
+        water_speed(n)
+        all_sent(f"pc{n}", (2, 3))
+        water_pressure()
         returning = receive_lists(f"t{n}", 2 * n + 1, traction)
         water_feed(returning)
         if n < STEPS - 1:
             sample = gather(W.at[0], rw, RW, LW) * FAC[...]
             send_lists(f"s{n + 1}", 2 * n + 2, sample)
             send_p(n + 1)
-        all_sent(f"s{n}", (0, 1))
-        all_sent(f"t{n}", (0, 1))
-        all_sent(f"ur{n}", (0, 1))
-        all_sent(f"vr{n}", (0, 1))
-        all_sent(f"vc{n}", (2, 3))
+    for name, d in list(pending):
+        sent(name, d)
 
 
 def store_kernel(water, steel, water_out, steel_out, sem):
@@ -431,7 +516,7 @@
     nh = nz // LANES
     vmem = pl.BlockSpec(memory_space=pltpu.VMEM)
     hbm = pl.BlockSpec(memory_space=pltpu.HBM)
-    rows_of = lambda fields: pltpu.VMEM((2, STEPS, fields, 1, nz), F32)
+    rows_of = lambda *lead: pltpu.VMEM((2, *lead, nh, LANES), F32)
     results = pl.pallas_call(
         functools.partial(kernel, (tiles, subs, rw, rs, nz, cap)),
         out_shape=(
@@ -456,21 +541,22 @@
             pltpu.VMEM((nh * rs, LANES), F32),
             pltpu.VMEM((2, 2 * STEPS, 1, cap), F32),
             pltpu.VMEM((2, 2 * STEPS, 1, cap), F32),
+            rows_of(STEPS, 5),
+            rows_of(STEPS, 5),
+            rows_of(3),
+            rows_of(3),
+            rows_of(STEPS, 2),
+            rows_of(STEPS, 2),
             rows_of(2),
             rows_of(2),
-            rows_of(2),
-            rows_of(2),
-            rows_of(1),
-            rows_of(1),
-            rows_of(1),
-            rows_of(1),
-            pltpu.VMEM((2, STEPS, 2, rs, LANES), F32),
-            pltpu.VMEM((2, STEPS, 2, rs, LANES), F32),
+            pltpu.VMEM((2, STEPS, 3, rs, LANES), F32),
+            pltpu.VMEM((2, 3, rs, LANES), F32),
             pltpu.VMEM((2, STEPS, rw, LANES), F32),
-            pltpu.VMEM((2, STEPS, rw, LANES), F32),
+            pltpu.VMEM((2, 2, rw, LANES), F32),
+            pltpu.VMEM((4, STEPS, 3, 8, LANES), F32),
             pltpu.SemaphoreType.DMA((9,)),
-            pltpu.SemaphoreType.DMA((64,)),
-            pltpu.SemaphoreType.DMA((64,)),
+            pltpu.SemaphoreType.DMA((80,)),
+            pltpu.SemaphoreType.DMA((80,)),
         ],
         compiler_params=pltpu.CompilerParams(
             collective_id=0, has_side_effects=True, vmem_limit_bytes=VMEM_BYTES - 4 * (water_state.size + steel_state.size)

time: 45.8 us -> 47.4 us (1.035)
  the two profiles are of different devices: /device:TPU:25 before, /device:TPU:28 now
where the time goes in v3:
time: 47.4 us; the launch traced here: 47.3 us
  Pallas kernels  46.7 us (99%)
  between operations  0.64 us (1%)
    pallas_call x1, Pallas kernels, on_device(): pl.pallas_call(functools.partial(kernel, (tiles, subs, rw, rs, nz, cap)),...  45.5 us
    pallas_call x1, Pallas kernels, on_device(): pl.pallas_call(store_kernel, out_shape=(jax.ShapeDtypeStruct(water_state....  1.2 us

profile of v3, /device:TPU:28, one launch (start us, length us, event | category | flops | bytes accessed | tf_op | source)
XLA Modules:
  0.0 47.3 jit_solution(17198656204978044514)
XLA Ops:
  0.6 45.5 %shard_map.104 = (f32[3,8,4096]{2,1,0:T(8,128)S(1)}, f32[5,16,4096]{2,1,0:T(8,128)S(1)}) custom-call(f32[9]{0:T(128)} %coupling_in.1, s32[1,3]{1,0:T(1,128)} %bitcast.1, s32[3,256]{1,0:T(4,128)} %water_cell_in.1, s32[3,256]{1,0:T(4,128)} %stencil_code_in.1, s32[3,256]{1,0:T(4,128)} %steel_cell_in.1, f32[3,8,4096]{2,1,0:T(8,128)} %water_in.1, ...), custom_call_target="tpu_custom_call" | custom-call | tf_op jit(solution)/shard_map/pallas_call | solution.py:520
  46.1 1.2 %shard_map.105 = (f32[3,8,4096]{2,1,0:T(8,128)}, f32[5,16,4096]{2,1,0:T(8,128)}) custom-call(f32[3,8,4096]{2,1,0:T(8,128)S(1)} %get-tuple-element.4.water, f32[5,16,4096]{2,1,0:T(8,128)S(1)} %get-tuple-element.5.steel), custom_call_target="tpu_custom_call" | custom-call | tf_op jit(solution)/shard_map/pallas_call | solution.py:575

commit v4 on v3

v4 whole, which is shorter than its diff:
```python
import functools

import jax
import jax.numpy as jnp
from jax import lax
from jax.experimental import pallas as pl
from jax.experimental.pallas import tpu as pltpu
from jax.sharding import PartitionSpec as P

MESH = pl.DeviceIdType.MESH
STEPS = 3
LANES = 128
VMEM_BYTES = 67043328
F32 = jnp.float32
BF16 = jnp.bfloat16


def split_two(x):
    first = x.astype(BF16)
    return first, (x - first.astype(F32)).astype(BF16)


class Columns:
    def __init__(self, get, left, right, count, shape):
        self.get, self.left, self.right, self.count = get, left, right, count
        lane = lax.broadcasted_iota(jnp.int32, shape, 1)
        self.is_first, self.is_last = lane == 0, lane == LANES - 1
        self.before, self.after = {}, {}

    def tile(self, h):
        return self.left() if h < 0 else self.right() if h == self.count else self.get(h)

    def rolled(self, h, cache, shift):
        if h not in cache:
            cache[h] = pltpu.roll(self.tile(h), shift, 1)
        return cache[h]

    def __call__(self, h):
        previous = jnp.where(
            self.is_first, self.rolled(h - 1, self.before, 1), self.rolled(h, self.before, 1)
        )
        following = jnp.where(
            self.is_last,
            self.rolled(h + 1, self.after, LANES - 1),
            self.rolled(h, self.after, LANES - 1),
        )
        return following - previous


def row_difference(tile, above, below, is_top, is_bottom):
    rows = tile.shape[0]
    previous = jnp.where(is_top, above, pltpu.roll(tile, 1, 0))
    following = jnp.where(is_bottom, below, pltpu.roll(tile, rows - 1, 0))
    return following - previous


def kernel(
    dims,
    coupling_in,
    counts_in,
    water_cell_in,
    stencil_code_in,
    steel_cell_in,
    water_in,
    water_coef_in,
    steel_in,
    steel_coef_in,
    W,
    S,
    coupling,
    counts,
    water_cell,
    stencil_code,
    steel_cell,
    WC,
    SC,
    RW,
    RS,
    LW,
    LS,
    FAC,
    LOAD,
    EQ,
    lists_out,
    lists_in,
    near_out,
    near_in,
    far_out,
    far_in,
    known_out,
    known_in,
    stress_rows_out,
    stress_rows_in,
    part_rows_out,
    part_rows_in,
    coef_rows_out,
    coef_rows_in,
    speed_rows,
    p_rows_out,
    p_rows_in,
    wcoef_rows_out,
    wcoef_rows_in,
    vx_rows,
    stress_cols_in,
    part_cols_in,
    coef_cols_in,
    speed_cols,
    p_cols_in,
    vz_cols_in,
    wcoef_cols_in,
    vz_cols,
    corners_in,
    local_sem,
    send_sem,
    recv_sem,
):
    tiles, subs, rw, rs, nz, cap = dims
    nh = nz // LANES
    shift = nz.bit_length() - 1
    slots = 3 * cap
    a = lax.axis_index("tile")
    c = lax.axis_index("sub")
    moves = ((-1, 0), (1, 0), (0, -1), (0, 1), (-1, -1), (-1, 1), (1, -1), (1, 1), (-2, 0), (2, 0))
    opposite = (1, 0, 3, 2, 7, 6, 5, 4, 9, 8)
    along = {
        (0, -1): c > 0,
        (0, 1): c < subs - 1,
        (-1, 0): a > 0,
        (1, 0): a < tiles - 1,
        (-2, 0): a > 1,
        (2, 0): a < tiles - 2,
    }
    has = [
        along[m] if m in along else jnp.logical_and(along[(m[0], 0)], along[(0, m[1])])
        for m in moves
    ]
    target = [(a + m[0], c + m[1]) for m in moves]

    barrier = pltpu.get_barrier_semaphore()
    for d in range(10):

        @pl.when(has[d])
        def _():
            pl.semaphore_signal(barrier, inc=1, device_id=target[d], device_id_type=MESH)

    loads = [
        pltpu.make_async_copy(src, dst, local_sem.at[i])
        for i, (src, dst) in enumerate(
            (
                (coupling_in, coupling),
                (counts_in, counts),
                (stencil_code_in, stencil_code),
                (water_cell_in, water_cell),
                (water_in, W),
                (steel_cell_in, steel_cell),
                (steel_in, S),
                (water_coef_in, WC),
                (steel_coef_in, SC),
            )
        )
    ]
    for load in loads:
        load.start()

    ids = {}

    def copy(name, d, src, dst):
        key = (name, d)
        if key not in ids:
            ids[key] = len(ids)
        return pltpu.make_async_remote_copy(
            src_ref=src,
            dst_ref=dst,
            send_sem=send_sem.at[ids[key]],
            recv_sem=recv_sem.at[ids[key]],
            device_id=target[d],
            device_id_type=MESH,
        )

    pending = {}

    def send(name, d, src, dst):
        @pl.when(has[d])
        def _():
            copy(name, d, src, dst).start()

        pending[(name, d)] = (src, dst)

    def arrived(name, d, dst):
        @pl.when(has[opposite[d]])
        def _():
            copy(name, d, dst, dst).wait_recv()

    def sent(name, d):
        src, dst = pending.pop((name, d))

        @pl.when(has[d])
        def _():
            copy(name, d, src, dst).wait_send()

    row_refs = (
        lists_in,
        near_in,
        known_in,
        stress_rows_in,
        part_rows_in,
        coef_rows_in,
        p_rows_in,
        wcoef_rows_in,
    )
    col_refs = (
        stress_cols_in,
        part_cols_in,
        coef_cols_in,
        p_cols_in,
        vz_cols_in,
        wcoef_cols_in,
    )
    for d in range(10):
        refs = row_refs if d < 2 else col_refs if d < 4 else (corners_in,) if d < 8 else (far_in,)

        @pl.when(jnp.logical_not(has[opposite[d]]))
        def _():
            for ref in refs:
                part = ref.at[d if d < 2 else d - 2 if d < 4 else d - 4 if d < 8 else d - 8]
                part[...] = jnp.zeros(part.shape, F32)

    for load in loads[:4]:
        load.wait()
    lane_row = lambda ref: jnp.concatenate([ref[0:1, :], ref[1:2, :], ref[2:3, :]], axis=1)
    wcell = lane_row(water_cell)
    code = lane_row(stencil_code)
    slot = lax.broadcasted_iota(jnp.int32, (1, cap), 1)
    live = jnp.concatenate([slot < counts[0, m] for m in range(3)], axis=1)
    weight = jnp.zeros((1, slots), F32)
    for k in range(9):
        weight = jnp.where(code == k, coupling[k], weight)
    FAC[...] = jnp.where(live, weight, 0.0)

    def selectors(cell, rows, R, L):
        row = cell >> shift
        key = ((cell >> 7) & (nh - 1)) * rows + row
        low = cell & (LANES - 1)
        count = nh * rows
        block = min(128, count)
        for k0 in range(0, count, block):
            index = lax.broadcasted_iota(jnp.int32, (block, slots), 0) + k0
            R[k0 : k0 + block, :] = jnp.where(index == key, 1.0, 0.0).astype(BF16)
        index = lax.broadcasted_iota(jnp.int32, (LANES, slots), 0)
        L[...] = jnp.where(index == low, 1.0, 0.0)

    selectors(wcell, rw, RW, LW)

    def gather(field, rows, R, L):
        stacked = jnp.concatenate(
            [field[:, h * LANES : (h + 1) * LANES] for h in range(nh)], axis=0
        )
        parts = split_two(jnp.transpose(stacked))
        picked = jnp.dot(
            jnp.concatenate(parts, axis=0), R[...], preferred_element_type=F32
        )
        picked = (picked[:LANES] + picked[LANES:]) * L[...]
        return jnp.sum(picked, axis=0, keepdims=True)

    def scatter(values, R, L):
        parts = split_two(L[...] * values)
        spread = lax.dot_general(
            R[...],
            jnp.concatenate(parts, axis=0),
            (((1,), (1,)), ((), ())),
            preferred_element_type=F32,
        )
        return spread[:, :LANES] + spread[:, LANES:]

    def masks(rows):
        row = lax.broadcasted_iota(jnp.int32, (rows, LANES), 0)
        return row == 0, row == rows - 1

    steel_top, steel_bottom = masks(rs)
    water_top, water_bottom = masks(rw)
    at = lambda h: slice(h * LANES, (h + 1) * LANES)

    def send_lists(name, n, values):
        lists_out[0, n] = values[:, :cap]
        lists_out[1, n] = values[:, 2 * cap :]
        for d in (0, 1):
            send(name, d, lists_out.at[d, n], lists_in.at[d, n])

    def wait_lists(name, n):
        for d in (0, 1):
            arrived(name, d, lists_in.at[d, n])

    def send_tractions(n, values):
        near_out[0, n] = values[:, : 2 * cap]
        near_out[1, n] = values[:, cap:]
        for d in (0, 1):
            send(f"t{n}", d, near_out.at[d, n], near_in.at[d, n])
        if n < STEPS - 1:
            far_out[0, n] = values[:, :cap]
            far_out[1, n] = values[:, 2 * cap :]
            for d in (8, 9):
                send(f"f{n}", d, far_out.at[d - 8, n], far_in.at[d - 8, n])

    def wait_tractions(n):
        for d in (0, 1):
            arrived(f"t{n}", d, near_in.at[d, n])
        if n < STEPS - 1:
            for d in (8, 9):
                arrived(f"f{n}", d, far_in.at[d - 8, n])

    first, last = slice(0, LANES), slice(nz - LANES, nz)

    def put_row(out, ref, f, r):
        for h in range(nh):
            out[h : h + 1, :] = ref[f, r : r + 1, at(h)]

    def put_rows(out, fields, rows):
        for d in (0, 1):
            for i, (ref, f) in enumerate(fields):
                put_row(out(d).at[i], ref, f, rows - 1 if d else 0)

    put_stress = lambda n: put_rows(lambda d: stress_rows_out.at[d, n], ((S, 2), (S, 4)), rs)
    put_part = lambda n: put_rows(lambda d: part_rows_out.at[d, n], ((S, 0), (S, 1)), rs)
    put_p = lambda n: put_rows(lambda d: p_rows_out.at[d, n, 0:1], ((W, 0),), rw)
    put_vx = lambda n: put_rows(lambda d: p_rows_out.at[d, n, 1:2], ((W, 1),), rw)

    edges = ((2, first), (3, last))
    all_rows = lambda name, out, into: [send(name, d, out(d), into(d)) for d in (0, 1)]
    all_cols = lambda name, src, into: [
        send(name, d, src(lanes), into(d - 2)) for d, lanes in edges
    ]

    def send_stress(n):
        all_rows(f"sr{n}", lambda d: stress_rows_out.at[d, n], lambda d: stress_rows_in.at[d, n])
        all_cols(f"sc{n}", lambda e: S.at[3:5, :, e], lambda d: stress_cols_in.at[d, n])
        for d in range(4, 8):
            rows = slice(0, 8) if moves[d][0] < 0 else slice(rs - 8, rs)
            lanes = first if moves[d][1] < 0 else last
            send(f"sd{n}", d, S.at[2:5, rows, lanes], corners_in.at[d - 4, n])

    def send_part(n):
        all_rows(f"ar{n}", lambda d: part_rows_out.at[d, n], lambda d: part_rows_in.at[d, n])
        all_cols(f"uc{n}", lambda e: S.at[0:2, :, e], lambda d: part_cols_in.at[d, n])

    def send_p(n):
        all_rows(f"pr{n}", lambda d: p_rows_out.at[d, n], lambda d: p_rows_in.at[d, n])
        all_cols(f"pc{n}", lambda e: W.at[0:1, :, e], lambda d: p_cols_in.at[d, n])
        all_cols(f"vc{n}", lambda e: W.at[2:3, :, e], lambda d: vz_cols_in.at[d, n])

    def wait_steel(n):
        for d in (0, 1):
            arrived(f"sr{n}", d, stress_rows_in.at[d, n])
        for d in (2, 3):
            arrived(f"sc{n}", d, stress_cols_in.at[d - 2, n])
        for d in range(4, 8):
            arrived(f"sd{n}", d, corners_in.at[d - 4, n])
        for d in (0, 1):
            arrived(f"ar{n}", d, part_rows_in.at[d, n])
        for d in (2, 3):
            arrived(f"uc{n}", d, part_cols_in.at[d - 2, n])

    def wait_water(n):
        for d in (0, 1):
            arrived(f"pr{n}", d, p_rows_in.at[d, n])
        for d in (2, 3):
            arrived(f"pc{n}", d, p_cols_in.at[d - 2, n])
            arrived(f"vc{n}", d, vz_cols_in.at[d - 2, n])

    def all_sent(name, directions):
        for d in directions:
            sent(name, d)

    def columns(ref, f, rows, into=None):
        zero = jnp.zeros((rows, LANES), F32)
        side = (lambda s: zero) if into is None else into
        return Columns(lambda h: ref[f, :, at(h)], lambda: side(1), lambda: side(0), nh, (rows, LANES))

    def rows_of(ref, f, top, bottom, into=None):
        side = lambda s, h: 0.0 if into is None else into(s)[h : h + 1, :]
        return lambda h: row_difference(ref[f, :, at(h)], side(1, h), side(0, h), top, bottom)

    line = lax.broadcasted_iota(jnp.int32, (nh, LANES), 0)
    lane = lax.broadcasted_iota(jnp.int32, (nh, LANES), 1)
    row_start = jnp.logical_and(line == 0, lane == 0)
    row_end = jnp.logical_and(line == nh - 1, lane == LANES - 1)

    def lanes_of(rows):
        index = lax.broadcasted_iota(jnp.int32, (rows, LANES), 1)
        return index == 0, index == LANES - 1

    back = lambda x: pltpu.roll(x, 1, 1)
    forth = lambda x: pltpu.roll(x, LANES - 1, 1)

    def outside_rows(above, below, top, bottom):
        return jnp.where(top, -above, jnp.where(bottom, below, 0.0))

    def outside_cols(h, rows, left, right):
        start, end = lanes_of(rows)
        if h == 0:
            return jnp.where(start, -back(left), 0.0)
        if h == nh - 1:
            return jnp.where(end, forth(right), 0.0)
        return None

    def corner(up, left, n, i):
        r = 7 if up else 0
        return corners_in[2 * up + left, n, i, r : r + 1, :]

    def outer_speed(n):
        for side in (1, 0):
            half = 0.5 * coef_rows_in[side, 0]
            for i, field in ((0, 2), (1, 1)):
                near = stress_rows_out[1 - side, n, i]
                change = jnp.where(row_end, forth(corner(side, 0, n, field)), 0.0) - jnp.where(
                    row_start, back(corner(side, 1, n, field)), 0.0
                )
                change = change + near if side else change - near
                speed_rows[side, i] = part_rows_in[side, n, i] + half * change
        for side in (1, 0):
            half = 0.5 * coef_cols_in[side, 0]
            for i, (down, flat) in enumerate(((0, 4), (2, 3))):
                change = outside_rows(
                    corner(1, side, n, down), corner(0, side, n, down), steel_top, steel_bottom
                )
                if side:
                    change = change + forth(S[flat, :, first])
                else:
                    change = change - back(S[flat, :, last])
                speed_cols[side, i] = part_cols_in[side, n, i] + half * change

    def steel_part():
        dr_xx = rows_of(S, 2, steel_top, steel_bottom)
        dr_xz = rows_of(S, 4, steel_top, steel_bottom)
        dc_zz = columns(S, 3, rs)
        dc_xz = columns(S, 4, rs)
        for h in range(nh):
            half = 0.5 * SC[0, :, at(h)]
            S[0, :, at(h)] = S[0, :, at(h)] + half * (dr_xx(h) + dc_xz(h))
            S[1, :, at(h)] = S[1, :, at(h)] + half * (dr_xz(h) + dc_zz(h))

    def steel_rest(n):
        for h in range(nh):
            half = 0.5 * SC[0, :, at(h)]
            changes = []
            for i, flat in ((0, 1), (1, 0)):
                change = outside_rows(
                    stress_rows_in[1, n, i, h : h + 1, :],
                    stress_rows_in[0, n, i, h : h + 1, :],
                    steel_top,
                    steel_bottom,
                )
                if h in (0, nh - 1):
                    change = change + outside_cols(
                        h, rs, stress_cols_in[1, n, flat], stress_cols_in[0, n, flat]
                    )
                changes.append(change)
            S[0, :, at(h)] = S[0, :, at(h)] + half * changes[0]
            S[1, :, at(h)] = S[1, :, at(h)] + half * (
                changes[1] - 2.0 * LOAD[h * rs : (h + 1) * rs, :]
            )

    def steel_stress():
        dr_x = rows_of(S, 0, steel_top, steel_bottom, lambda side: speed_rows.at[side, 0])
        dr_z = rows_of(S, 1, steel_top, steel_bottom, lambda side: speed_rows.at[side, 1])
        dc_x = columns(S, 0, rs, lambda side: speed_cols[side, 0])
        dc_z = columns(S, 1, rs, lambda side: speed_cols[side, 1])
        for h in range(nh):
            across, along = 0.5 * dr_x(h), 0.5 * dc_z(h)
            S[2, :, at(h)] = S[2, :, at(h)] + SC[1, :, at(h)] * across + SC[2, :, at(h)] * along
            S[3, :, at(h)] = S[3, :, at(h)] + SC[2, :, at(h)] * across + SC[3, :, at(h)] * along
            S[4, :, at(h)] = S[4, :, at(h)] + (0.5 * SC[4, :, at(h)]) * (dc_x(h) + dr_z(h))

    def water_part():
        dr_p = rows_of(W, 0, water_top, water_bottom)
        dc_p = columns(W, 0, rw)
        for h in range(nh):
            half = 0.5 * WC[0, :, at(h)]
            W[1, :, at(h)] = W[1, :, at(h)] - half * dr_p(h)
            W[2, :, at(h)] = W[2, :, at(h)] - half * dc_p(h)

    def water_rest(n):
        for side in (1, 0):
            near = p_rows_out[1 - side, n, 0]
            half = 0.5 * wcoef_rows_in[side, 0]
            vx_rows[side] = p_rows_in[side, n, 1] - half * (near if side else -near)
            half = 0.5 * wcoef_cols_in[side, 0]
            beside = forth(W[0, :, first]) if side else -back(W[0, :, last])
            vz_cols[side] = vz_cols_in[side, n, 0] - half * beside
        for h in range(nh):
            half = 0.5 * WC[0, :, at(h)]
            W[1, :, at(h)] = W[1, :, at(h)] - half * outside_rows(
                p_rows_in[1, n, 0, h : h + 1, :],
                p_rows_in[0, n, 0, h : h + 1, :],
                water_top,
                water_bottom,
            )
            if h in (0, nh - 1):
                W[2, :, at(h)] = W[2, :, at(h)] - half * outside_cols(
                    h, rw, p_cols_in[1, n, 0], p_cols_in[0, n, 0]
                )

    def water_pressure():
        dr_v = rows_of(W, 1, water_top, water_bottom, lambda side: vx_rows.at[side])
        dc_v = columns(W, 2, rw, lambda side: vz_cols[side])
        for h in range(nh):
            W[0, :, at(h)] = W[0, :, at(h)] - (0.5 * WC[1, :, at(h)]) * (dr_v(h) + dc_v(h))

    def water_feed(values):
        fed = scatter(values, RW, LW)
        for h in range(nh):
            W[0, :, at(h)] = W[0, :, at(h)] + fed[h * rw : (h + 1) * rw, :]

    def equal_cells(i, cells, start):
        for s0 in range(0, cap, LANES):
            block = cells[:, start + s0 : start + s0 + LANES]
            down = jnp.transpose(jnp.broadcast_to(block, (LANES, LANES)))
            for t0 in range(0, slots, LANES):
                same = down == cells[:, t0 : t0 + LANES]
                EQ[i, s0 : s0 + LANES, t0 : t0 + LANES] = jnp.where(same, 1.0, 0.0).astype(BF16)

    def fed_at_slots(i, values):
        high, low = split_two(values)
        upper = lax.broadcasted_iota(jnp.int32, (16, slots), 0) < 8
        both = jnp.where(upper, high.astype(F32), low.astype(F32)).astype(BF16)
        out = lax.dot_general(
            both, EQ[i], (((1,), (1,)), ((), ())), preferred_element_type=F32
        )
        return out[0:1] + out[8:9]

    loads[4].wait()
    sample = gather(W.at[0], rw, RW, LW) * FAC[...]
    known_out[0] = wcell.astype(F32)
    known_out[1] = FAC[...]
    loads[6].wait()
    loads[8].wait()
    put_stress(0)
    put_rows(lambda d: coef_rows_out.at[d], ((SC, 0),), rs)
    steel_part()
    put_part(0)
    loads[7].wait()
    put_p(0)
    put_rows(lambda d: wcoef_rows_out.at[d], ((WC, 0),), rw)
    water_part()
    put_vx(0)
    loads[5].wait()
    selectors(lane_row(steel_cell), rs, RS, LS)
    pl.semaphore_wait(barrier, sum(h.astype(jnp.int32) for h in has))
    send_lists("s0", 0, sample)
    for d in (0, 1):
        send("k", d, known_out, known_in.at[d])
    send_stress(0)
    send_part(0)
    all_rows("br", lambda d: coef_rows_out.at[d], lambda d: coef_rows_in.at[d])
    all_cols("bc", lambda e: SC.at[0:1, :, e], lambda d: coef_cols_in.at[d])
    send_p(0)
    all_rows("wr", lambda d: wcoef_rows_out.at[d], lambda d: wcoef_rows_in.at[d])
    all_cols("wc", lambda e: WC.at[0:1, :, e], lambda d: wcoef_cols_in.at[d])
    equal_cells(1, wcell.astype(F32), cap)
    wait_lists("s0", 0)
    loading = jnp.concatenate([lists_in[1, 0], sample[:, cap : 2 * cap], lists_in[0, 0]], axis=1)
    for d in (0, 1):
        arrived("k", d, known_in.at[d])
    equal_cells(0, known_in[1, 0], 2 * cap)
    equal_cells(2, known_in[0, 0], 0)
    for n in range(STEPS):
        LOAD[...] = scatter(loading, RS, LS)
        wait_steel(n)
        if n == 0:
            for d in (0, 1):
                arrived("br", d, coef_rows_in.at[d])
            for d in (2, 3):
                arrived("bc", d, coef_cols_in.at[d - 2])
        outer_speed(n)
        all_sent(f"uc{n}", (2, 3))
        steel_rest(n)
        all_sent(f"sc{n}", (2, 3))
        all_sent(f"sd{n}", range(4, 8))
        steel_stress()
        traction = gather(S.at[3], rs, RS, LS)
        send_tractions(n, traction)
        if n < STEPS - 1:
            put_stress(n + 1)
            send_stress(n + 1)
            steel_part()
            put_part(n + 1)
            send_part(n + 1)
        wait_water(n)
        if n == 0:
            for d in (0, 1):
                arrived("wr", d, wcoef_rows_in.at[d])
            for d in (2, 3):
                arrived("wc", d, wcoef_cols_in.at[d - 2])
        all_sent(f"vc{n}", (2, 3))
        water_rest(n)
        all_sent(f"pc{n}", (2, 3))
        water_pressure()
        if n < STEPS - 1:
            unfed = gather(W.at[0], rw, RW, LW)
            send_lists(f"q{n + 1}", n + 1, unfed)
        wait_tractions(n)
        own = FAC[...] * jnp.concatenate(
            [
                near_in[1, n][:, cap:],
                traction[:, cap : 2 * cap],
                near_in[0, n][:, :cap],
            ],
            axis=1,
        )
        water_feed(own)
        if n < STEPS - 1:
            put_p(n + 1)
            water_part()
            put_vx(n + 1)
            send_p(n + 1)
            before = known_in[1, 1] * jnp.concatenate(
                [far_in[1, n], near_in[1, n][:, :cap], traction[:, :cap]], axis=1
            )
            after = known_in[0, 1] * jnp.concatenate(
                [traction[:, 2 * cap :], near_in[0, n][:, cap:], far_in[0, n]], axis=1
            )
            fed = [fed_at_slots(i, v) for i, v in enumerate((before, own, after))]
            wait_lists(f"q{n + 1}", n + 1)
            loading = jnp.concatenate(
                [
                    known_in[1, 1][:, 2 * cap :] * (lists_in[1, n + 1] + fed[0]),
                    FAC[:, cap : 2 * cap] * (unfed[:, cap : 2 * cap] + fed[1]),
                    known_in[0, 1][:, :cap] * (lists_in[0, n + 1] + fed[2]),
                ],
                axis=1,
            )
    for name, d in list(pending):
        sent(name, d)


def store_kernel(water, steel, water_out, steel_out, sem):
    stores = [
        pltpu.make_async_copy(steel, steel_out, sem.at[0]),
        pltpu.make_async_copy(water, water_out, sem.at[1]),
    ]
    for store in stores:
        store.start()
    for store in stores:
        store.wait()


def on_device(
    tiles,
    subs,
    water_state,
    water_coef,
    steel_state,
    steel_coef,
    coupling,
    water_cell,
    stencil_code,
    link_count,
    steel_cell,
):
    rw, nz = water_state.shape[1:]
    rs = steel_state.shape[1]
    cap = water_cell.shape[1]
    slots = 3 * cap
    nh = nz // LANES
    vmem = pl.BlockSpec(memory_space=pltpu.VMEM)
    hbm = pl.BlockSpec(memory_space=pltpu.HBM)
    rows_of = lambda *lead: pltpu.VMEM((2, *lead, nh, LANES), F32)
    results = pl.pallas_call(
        functools.partial(kernel, (tiles, subs, rw, rs, nz, cap)),
        out_shape=(
            pltpu.VMEM(water_state.shape, F32),
            pltpu.VMEM(steel_state.shape, F32),
        ),
        in_specs=[hbm] * 9,
        out_specs=(vmem, vmem),
        scratch_shapes=[
            pltpu.SMEM(coupling.shape, F32),
            pltpu.SMEM((1, 3), jnp.int32),
            pltpu.VMEM(water_cell.shape, jnp.int32),
            pltpu.VMEM(water_cell.shape, jnp.int32),
            pltpu.VMEM(water_cell.shape, jnp.int32),
            pltpu.VMEM(water_coef.shape, F32),
            pltpu.VMEM(steel_coef.shape, F32),
            pltpu.VMEM((nh * rw, slots), BF16),
            pltpu.VMEM((nh * rs, slots), BF16),
            pltpu.VMEM((LANES, slots), F32),
            pltpu.VMEM((LANES, slots), F32),
            pltpu.VMEM((1, slots), F32),
            pltpu.VMEM((nh * rs, LANES), F32),
            pltpu.VMEM((3, cap, slots), BF16),
            pltpu.VMEM((2, STEPS, 1, cap), F32),
            pltpu.VMEM((2, STEPS, 1, cap), F32),
            pltpu.VMEM((2, STEPS, 1, 2 * cap), F32),
            pltpu.VMEM((2, STEPS, 1, 2 * cap), F32),
            pltpu.VMEM((2, STEPS, 1, cap), F32),
            pltpu.VMEM((2, STEPS, 1, cap), F32),
            pltpu.VMEM((2, 1, slots), F32),
            pltpu.VMEM((2, 2, 1, slots), F32),
            rows_of(STEPS, 2),
            rows_of(STEPS, 2),
            rows_of(STEPS, 2),
            rows_of(STEPS, 2),
            rows_of(1),
            rows_of(1),
            rows_of(2),
            rows_of(STEPS, 2),
            rows_of(STEPS, 2),
            rows_of(1),
            rows_of(1),
            rows_of(),
            pltpu.VMEM((2, STEPS, 2, rs, LANES), F32),
            pltpu.VMEM((2, STEPS, 2, rs, LANES), F32),
            pltpu.VMEM((2, 1, rs, LANES), F32),
            pltpu.VMEM((2, 2, rs, LANES), F32),
            pltpu.VMEM((2, STEPS, 1, rw, LANES), F32),
            pltpu.VMEM((2, STEPS, 1, rw, LANES), F32),
            pltpu.VMEM((2, 1, rw, LANES), F32),
            pltpu.VMEM((2, rw, LANES), F32),
            pltpu.VMEM((4, STEPS, 3, 8, LANES), F32),
            pltpu.SemaphoreType.DMA((9,)),
            pltpu.SemaphoreType.DMA((96,)),
            pltpu.SemaphoreType.DMA((96,)),
        ],
        compiler_params=pltpu.CompilerParams(
            collective_id=0, has_side_effects=True, vmem_limit_bytes=VMEM_BYTES - 4 * (water_state.size + steel_state.size)
        ),
    )(
        coupling,
        link_count.reshape(1, 3),
        water_cell,
        stencil_code,
        steel_cell,
        water_state,
        water_coef,
        steel_state,
        steel_coef,
    )
    return pl.pallas_call(
        store_kernel,
        out_shape=(
            jax.ShapeDtypeStruct(water_state.shape, F32),
            jax.ShapeDtypeStruct(steel_state.shape, F32),
        ),
        in_specs=[vmem, vmem],
        out_specs=(hbm, hbm),
        scratch_shapes=[pltpu.SemaphoreType.DMA((2,))],
        compiler_params=pltpu.CompilerParams(vmem_limit_bytes=1024 * 1024),
    )(*results)


def solution(mesh):
    in_specs = (
        P(None, "tile", "sub"),
        P(None, "tile", "sub"),
        P(None, "tile", "sub"),
        P(None, "tile", "sub"),
        P(),
        P("tile", "sub"),
        P("tile", "sub"),
        P("tile", "sub"),
        P("tile", "sub"),
    )
    out_specs = (P(None, "tile", "sub"), P(None, "tile", "sub"))
    return jax.shard_map(
        functools.partial(on_device, mesh.shape["tile"], mesh.shape["sub"]),
        mesh=mesh,
        in_specs=in_specs,
        out_specs=out_specs,
        check_vma=False,
    )
```

time: 47.4 us -> 40 us (0.84)
  the two profiles are of different devices: /device:TPU:28 before, /device:TPU:25 now
where the time goes in v4:
time: 40 us; the launch traced here: 39.5 us
  Pallas kernels  38.9 us (97%)
  between operations  0.64 us (2%)
    pallas_call x1, Pallas kernels, on_device(): pl.pallas_call(functools.partial(kernel, (tiles, subs, rw, rs, nz, cap)),...  37.7 us
    pallas_call x1, Pallas kernels, on_device(): pl.pallas_call(store_kernel, out_shape=(jax.ShapeDtypeStruct(water_state....  1.2 us

profile of v4, /device:TPU:25, one launch (start us, length us, event | category | flops | bytes accessed | tf_op | source)
XLA Modules:
  0.0 39.5 jit_solution(12616864368542863342)
XLA Ops:
  0.6 37.7 %shard_map.104 = (f32[3,8,4096]{2,1,0:T(8,128)S(1)}, f32[5,16,4096]{2,1,0:T(8,128)S(1)}) custom-call(f32[9]{0:T(128)} %coupling_in.1, s32[1,3]{1,0:T(1,128)} %bitcast.1, s32[3,256]{1,0:T(4,128)} %water_cell_in.1, s32[3,256]{1,0:T(4,128)} %stencil_code_in.1, s32[3,256]{1,0:T(4,128)} %steel_cell_in.1, f32[3,8,4096]{2,1,0:T(8,128)} %water_in.1, ...), custom_call_target="tpu_custom_call" | custom-call | tf_op jit(solution)/shard_map/pallas_call | solution.py:667
  38.3 1.2 %shard_map.105 = (f32[3,8,4096]{2,1,0:T(8,128)}, f32[5,16,4096]{2,1,0:T(8,128)}) custom-call(f32[3,8,4096]{2,1,0:T(8,128)S(1)} %get-tuple-element.4.water, f32[5,16,4096]{2,1,0:T(8,128)S(1)} %get-tuple-element.5.steel), custom_call_target="tpu_custom_call" | custom-call | tf_op jit(solution)/shard_map/pallas_call | solution.py:737
